TPU v7x, 512 devices: a whole 4x4x16 slice. The times are simulated.
512 devices in a mesh: dp: 128 (over z, x, core), mp: 4 (over y).
Axes of the slice: x: 4, y: 4, z: 16, core: 2. Of those that a mesh axis runs over, the one named last changes fastest.
Arguments:
- query_states: bfloat16 [16384, 1024], P('dp'), may hold values from -41 to 41
- passage_states: bfloat16 [16384, 1024], P('dp'), may hold values from -41 to 41
- w_in: bfloat16 [1024, 4096], P(None, 'mp'), may hold values from -0.1875 to 0.1875
- w_out: bfloat16 [4096, 1024], P('mp'), may hold values from -0.09375 to 0.09375
- neg_owner: int32 [16384, 8], P('dp'), may hold values from 0 to 127, all different within a row; in each aligned block of 128 rows (0 to 127, 128 to 255, ...) at most 16 rows name the same one
- neg_mask: int32 [16384, 8], P('dp'), may hold values 0 or 1
- served_rows: int32 [128, 128, 16], P('dp'), may hold values from 0 to 127
- loss_scale: float32 [], replicated, may hold values from 32 to 128
Outputs:
- grad_query_states: bfloat16 [16384, 1024], P('dp', 'mp')
- grad_passage_states: bfloat16 [16384, 1024], P('dp', 'mp')
Inputs may be any that keep to these rules, and one draw needn't show every extreme that they name: Within the queries of one owner (aligned blocks of 128 rows) no owner is named by more than 16 entries of neg_owner, and in some block one owner is named exactly 16 times; the 8 owners of one query are distinct.
All inputs are finite; a program needn't handle non-finite values. No bound on the sum of `neg_mask` on one device may be relied on, other than what follows from the above.
Results may differ from a plain program's by a relative error of at most 0.017.
Values may be sent and summed in bfloat16 or wider, within the bound.
A program may use at most 64 MiB of HBM per device.

v0:
```python
import jax
import jax.numpy as jnp
from jax import lax
from jax.sharding import PartitionSpec as P

logit_scale = 50.0
norm_eps = 1e-06
root_half = 0.7071067811865476
inv_root_two_pi = 0.3989422804014327


def gelu_value(values):
    return 0.5 * values * (1.0 + lax.erf(values * root_half))


def gelu_slope(values):
    return (
        0.5 * (1.0 + lax.erf(values * root_half))
        + values * jnp.exp(-0.5 * values * values) * inv_root_two_pi
    )


def own_columns(values):
    column_width = values.shape[1] // lax.axis_size("mp")
    return lax.dynamic_slice_in_dim(values, lax.axis_index("mp") * column_width, column_width, 1)


def encode(states, w_in, w_out):
    pre_act = jnp.dot(states, w_in, preferred_element_type=jnp.float32)
    hidden = gelu_value(pre_act).astype(jnp.bfloat16)
    partial_out = jnp.dot(hidden, w_out, preferred_element_type=jnp.float32)
    mixed_sum = lax.psum(partial_out, "mp")
    output = states.astype(jnp.float32) + mixed_sum
    inv_norm = lax.rsqrt(jnp.sum(output * output, axis=1, keepdims=True) + norm_eps)
    return (pre_act, output * inv_norm, inv_norm)


def decode(grad_part, pre_act, unit_rows, inv_norm, w_in, w_out):
    grad_emb = lax.all_gather(grad_part.astype(jnp.bfloat16), "mp", axis=1, tiled=True).astype(
        grad_part.dtype
    )
    grad_out = inv_norm * (
        grad_emb - unit_rows * jnp.sum(unit_rows * grad_emb, axis=1, keepdims=True)
    )
    contract = (((1,), (1,)), ((), ()))
    grad_hidden = lax.dot_general(
        grad_out.astype(jnp.bfloat16), w_out, contract, preferred_element_type=jnp.float32
    )
    grad_pre = (grad_hidden * gelu_slope(pre_act)).astype(jnp.bfloat16)
    partial_in = lax.dot_general(grad_pre, w_in, contract, preferred_element_type=jnp.float32)
    summed = lax.psum_scatter(
        partial_in.astype(jnp.bfloat16), "mp", scatter_dimension=1, tiled=True
    ).astype(jnp.float32)
    return (summed + own_columns(grad_out)).astype(jnp.bfloat16)


def shards(query_states, passage_states, w_in, w_out, neg_owner, neg_mask, served_rows, loss_scale):
    owners = lax.axis_size("dp")
    row_count = query_states.shape[0]
    negatives = neg_owner.shape[1]
    capacity = served_rows.shape[2]
    pre_pass, unit_pass, inv_pass = encode(passage_states, w_in, w_out)
    emb_pass = own_columns(unit_pass).astype(jnp.bfloat16)
    column_width = emb_pass.shape[1]
    served = served_rows[0]
    flat_owner = neg_owner.reshape(-1)
    onehot = (flat_owner[:, None] == jnp.arange(owners, dtype=jnp.int32)[None, :]).astype(jnp.int32)
    before = jnp.cumsum(onehot, axis=0, dtype=jnp.int32) - onehot
    slot_index = jnp.sum(before * onehot, axis=1, dtype=jnp.int32)
    slot_place = flat_owner * capacity + slot_index
    every_emb = lax.all_gather(emb_pass, "dp", axis=0, tiled=True)
    rows_for_me = lax.all_to_all(
        served_rows, "dp", split_axis=1, concat_axis=0, tiled=True
    ).reshape(owners * capacity)
    neg_rows = jnp.take(rows_for_me, slot_place, axis=0)
    neg_emb = jnp.take(every_emb, flat_owner * row_count + neg_rows, axis=0)
    neg_emb = neg_emb.reshape(row_count, negatives, column_width)
    pre_query, unit_query, inv_query = encode(query_states, w_in, w_out)
    emb_query = own_columns(unit_query).astype(jnp.bfloat16)
    pos_part = jnp.einsum("qd,qd->q", emb_query, emb_pass, preferred_element_type=jnp.float32)
    neg_part = jnp.einsum("qd,qnd->qn", emb_query, neg_emb, preferred_element_type=jnp.float32)
    pos_score, neg_score = lax.psum((pos_part, neg_part), "mp")
    exp_pos = jnp.exp(logit_scale * pos_score)
    exp_neg = neg_mask.astype(jnp.float32) * jnp.exp(logit_scale * neg_score)
    denominator = exp_pos + jnp.sum(exp_neg, axis=1)
    factor = loss_scale * logit_scale
    grad_pos = factor * (exp_pos / denominator - 1.0)
    grad_neg = factor * exp_neg / denominator[:, None]
    query_values = emb_query.astype(jnp.float32)
    grad_query_emb = grad_pos[:, None] * emb_pass.astype(jnp.float32) + jnp.sum(
        grad_neg[:, :, None] * neg_emb.astype(jnp.float32), axis=1
    )
    slot_terms = (
        (grad_neg[:, :, None] * query_values[:, None, :])
        .astype(jnp.bfloat16)
        .reshape(-1, column_width)
    )
    outgoing_grad = (
        jnp.zeros((owners * capacity, column_width), jnp.bfloat16).at[slot_place].set(slot_terms)
    )
    returned = lax.all_to_all(
        outgoing_grad.reshape(owners, capacity, column_width),
        "dp",
        split_axis=0,
        concat_axis=0,
        tiled=True,
    )
    grad_query_states = decode(grad_query_emb, pre_query, unit_query, inv_query, w_in, w_out)
    gathered_back = (
        jnp.zeros((row_count, column_width), jnp.float32)
        .at[served.reshape(-1)]
        .add(returned.reshape(-1, column_width).astype(jnp.float32))
    )
    grad_pass_emb = grad_pos[:, None] * query_values + gathered_back
    grad_passage_states = decode(grad_pass_emb, pre_pass, unit_pass, inv_pass, w_in, w_out)
    return (grad_query_states, grad_passage_states)


def solution(mesh):
    in_specs = (
        P("dp", None),
        P("dp", None),
        P(None, "mp"),
        P("mp", None),
        P("dp", None),
        P("dp", None),
        P("dp", None, None),
        P(),
    )
    out_specs = (P("dp", "mp"), P("dp", "mp"))
    return jax.shard_map(shards, mesh=mesh, in_specs=in_specs, out_specs=out_specs, check_vma=False)
```

profile of v0, /device:TPU:4, one launch (start us, length us, event | category | flops | bytes accessed | tf_op | source)
XLA Modules:
  0.0 382.8 jit_solution(5777081302605767736)
XLA Ops:
  7.2 2.3 fusion.66
  10.2 0.8 copy-done.2
  11.0 1.3 fusion.34
  12.3 1.3 fusion.33
  13.7 66.0 %all-reduce.4.cloned.1.call-done = (f32[128,1024]{1,0:T(8,128)}, f32[128,1024]{1,0:T(8,128)}) async-done(((f32[128,1024]{1,0:T(8,128)}, f32[128,1024]{1,0:T(8,128)}), (f32[128,1024]{1,0:T(8,128)}, f32[128,1024]{1,0:T(8,128)})) %all-reduce.4.cloned.1.call-update) | async-done | bytes 1048592 | tf_op jit(solution)/shard_map/psum | solution.py:32
  79.7 1.5 multiply_reduce_fusion.1
  81.2 1.1 fusion.32
  82.4 1.1 fusion.31
  83.5 1.2 fusion.49
  85.4 16.5 %all-to-all-start = ((s32[1,128,16]{2,0,1:T(1,128)}), s32[1,128,16]{2,0,1:T(1,128)S(1)}, u32[]{:S(2)}, u32[]{:S(2)}) async-start(s32[1,128,16]{2,0,1:T(1,128)} %copy.37), calls=%async_computation | async-start | bytes 131072 | tf_op jit(solution)/shard_map/all_to_all | solution.py:72
  104.1 1.1 broadcast_add_fusion
  109.2 6.5 %all-to-all-done = s32[1,128,16]{2,0,1:T(1,128)S(1)} async-done(((s32[1,128,16]{2,0,1:T(1,128)}), s32[1,128,16]{2,0,1:T(1,128)S(1)}, u32[]{:S(2)}, u32[]{:S(2)}) %all-to-all-start) | async-done | bytes 8224 | tf_op jit(solution)/shard_map/all_to_all | solution.py:72
  116.2 0.8 reduce.5
  117.1 6.3 %gather_fusion = s32[1024]{0:T(1024)S(1)} fusion(s32[2048]{0:T(1024)S(1)} %reshape.189, s32[1024]{0:T(1024)} %broadcast_clamp_fusion.1), kind=kCustom, calls=%fused_computation | custom fusion | bytes 12288 | tf_op jit(solution)/shard_map/jit(_take)/gather | solution.py:75
  123.7 107.9 %all-gather.2.cloned.1.call-done = bf16[16384,256]{1,0:T(8,128)(2,1)} async-done(((bf16[128,256]{1,0:T(8,128)(2,1)}), bf16[16384,256]{1,0:T(8,128)(2,1)}) %all-gather.2.cloned.1.call-update) | async-done | bytes 8388624 | tf_op jit(solution)/shard_map/all_gather | solution.py:71
  231.6 9.0 %gather_fusion.1 = bf16[1024,256]{1,0:T(8,128)(2,1)} fusion(bf16[16384,256]{1,0:T(8,128)(2,1)} %all-gather.2.cloned.1.call-done, s32[1024]{0:T(1024)S(1)} %broadcast_clamp_fusion), kind=kCustom, calls=%fused_computation.1 | custom fusion | bytes 1052672 | tf_op jit(solution)/shard_map/jit(_take)/gather | solution.py:76
  240.6 1.4 fusion.30
  242.0 10.6 %all-reduce = (f32[128,8]{0,1:T(8,128)S(1)}, f32[128]{0:T(128)S(1)}) all-reduce(f32[128,8]{0,1:T(8,128)S(1)} %bitcast.48, f32[128]{0:T(128)S(1)} %copy-done.19), channel_id=1, replica_groups=mesh['dp'=128,'mp'=4] {'mp'}, use_global_device_ids=true, to_apply=%region_8.9 | all-reduce | flops 1152 | bytes 9216 | tf_op jit(solution)/shard_map/psum | solution.py:82
  252.9 6.5 %scatter_custom_fusion = bf16[2048,256]{1,0:T(8,128)(2,1)} fusion(s32[1024]{0:T(1024)S(1)} %bitcast.46, f32[128,256]{1,0:T(8,128)S(1)} %get-tuple-element.6, f32[1024]{0:T(1024)S(1)} %mul.280, bf16[]{:T(256)} %constant.75.clone.1), kind=kCustom, calls=%fused_computation.33 | custom fusion | flops 524288 | bytes 1183746 | tf_op jit(solution)/shard_map/scatter | solution.py:99
  259.4 12.0 %all-to-all-start.1 = ((bf16[128,16,256]{2,1,0:T(8,128)(2,1)}), bf16[128,16,256]{2,1,0:T(8,128)(2,1)}, u32[]{:S(2)}, u32[]{:S(2)}) async-start(bf16[128,16,256]{2,1,0:T(8,128)(2,1)} %bitcast.42), calls=%async_computation.2 | async-start | bytes 2097152 | tf_op jit(solution)/shard_map/all_to_all | solution.py:101
  271.7 1.5 multiply_reduce_fusion
  273.3 12.5 %all_gather.10 = bf16[128,1024]{1,0:T(8,128)(2,1)S(1)} all-gather(bf16[128,256]{1,0:T(8,128)(2,1)S(1)} %get-tuple-element.15), channel_id=1, replica_groups=mesh['dp'=128,'mp'=4] {'mp'}, dimensions={1}, use_global_device_ids=true | all-gather | bytes 327680 | tf_op jit(solution)/shard_map/all_gather | solution.py:39
  286.0 0.9 fusion.6
  286.9 4.2 %convolution_convert_fusion.1 = bf16[128,1024]{1,0:T(8,128)(2,1)} fusion(bf16[1024,1024]{1,0:T(8,128)(2,1)} %param.10, bf16[1024,1024]{1,0:T(8,128)(2,1)S(1)} %copy-done, f32[128,1024]{1,0:T(8,128)} %copy-done.4, f32[128,1024]{1,0:T(8,128)} %fusion.6), kind=kOutput, calls=%fused_computation.9 | convolution fusion | flops 538443776 | bytes 5505024 | tf_op jit(solution)/shard_map/dot_general | solution.py:50
  291.2 33.3 %all-to-all-done.1 = bf16[128,16,256]{2,1,0:T(8,128)(2,1)} async-done(((bf16[128,16,256]{2,1,0:T(8,128)(2,1)}), bf16[128,16,256]{2,1,0:T(8,128)(2,1)}, u32[]{:S(2)}, u32[]{:S(2)}) %all-to-all-start.1) | async-done | bytes 1048608 | tf_op jit(solution)/shard_map/all_to_all | solution.py:101
  324.5 12.1 %scatter_custom_fusion.1 = f32[128,256]{1,0:T(8,128)S(1)} fusion(f32[128,256]{1,0:T(8,128)S(1)} %get-tuple-element.14, s32[2048]{0:T(1024)S(1)} %bitcast.50, bf16[2048,256]{1,0:T(8,128)(2,1)} %bitcast.15), kind=kCustom, calls=%fused_computation.4 | custom fusion | flops 1048576 | bytes 1179648 | tf_op jit(solution)/shard_map/scatter-add | solution.py:112
  336.6 12.4 %all_gather.11 = bf16[128,1024]{1,0:T(8,128)(2,1)S(1)} all-gather(bf16[128,256]{1,0:T(8,128)(2,1)S(1)} %convert_element_type.111), channel_id=1, replica_groups=mesh['dp'=128,'mp'=4] {'mp'}, dimensions={1}, use_global_device_ids=true | all-gather | bytes 327680 | tf_op jit(solution)/shard_map/all_gather | solution.py:39
  349.1 0.9 fusion.8
  350.0 4.0 %convolution_convert_fusion = bf16[128,1024]{1,0:T(8,128)(2,1)} fusion(bf16[1024,1024]{1,0:T(8,128)(2,1)} %param.10, bf16[1024,1024]{1,0:T(8,128)(2,1)S(1)} %copy-done, f32[128,1024]{1,0:T(8,128)S(1)} %copy-done.3, f32[128,1024]{1,0:T(8,128)} %fusion.8), kind=kOutput, calls=%fused_computation.8 | convolution fusion | flops 538443776 | bytes 5505024 | tf_op jit(solution)/shard_map/dot_general | solution.py:50
  354.1 1.6 add_convert_fusion.1
  355.6 19.1 %reduce-scatter.5.cloned.1.call-done = bf16[128,256]{1,0:T(8,128)(2,1)} async-done(((bf16[128,1024]{1,0:T(8,128)(2,1)}), bf16[128,256]{1,0:T(8,128)(2,1)}) %reduce-scatter.5.cloned.1.call-update) | async-done | bytes 65552 | tf_op jit(solution)/shard_map/reduce_scatter | solution.py:51
  374.7 1.5 add_convert_fusion
  (93 shorter events, 9.0 us)
Async XLA Ops:
  7.2 3.8 %copy-start = (bf16[1024,1024]{1,0:T(8,128)(2,1)S(1)}, bf16[1024,1024]{1,0:T(8,128)(2,1)}, u32[]{:S(2)}) copy-start(bf16[1024,1024]{1,0:T(8,128)(2,1)} %param.11) | copy-start | bytes 6291460
  7.2 2.3 copy-start.5
  7.2 72.5 %all-reduce.4.cloned.1.call-start = ((), (), s32[]{:S(2)}) async-start(), calls=%async_computation.7 | async-start | bytes 2097152 | tf_op jit(solution)/shard_map/psum | solution.py:32
  7.2 2.5 copy-start.1
  9.7 2.6 copy-start.4
  10.2 0.8 copy-start.2
  12.3 67.4 %copy-start.6 = (bf16[128,1024]{1,0:T(8,128)(2,1)S(1)}, bf16[128,1024]{1,0:T(8,128)(2,1)}, u32[]{:S(2)}) copy-start(bf16[128,1024]{1,0:T(8,128)(2,1)} %param.8) | copy-start | bytes 786436
  13.6 218.0 %all-gather.2.cloned.1.call-start = ((), (), s32[]{:S(2)}) async-start(), calls=%async_computation.4 | async-start | bytes 8454144 | tf_op jit(solution)/shard_map/all_gather | solution.py:71
  79.7 2.7 copy-start.8
  79.7 5.0 %copy-start.11 = (s32[1,128,16]{1,2,0:T(8,128)S(1)}, s32[1,128,16]{1,2,0:T(8,128)}, u32[]{:S(2)}) copy-start(s32[1,128,16]{1,2,0:T(8,128)} %param.14) | copy-start | bytes 24580
  79.7 22.2 %copy-start.10 = (s32[128,8]{0,1:T(8,128)S(1)}, s32[128,8]{0,1:T(8,128)}, u32[]{:S(2)}) copy-start(s32[128,8]{0,1:T(8,128)} %param.12) | copy-start | bytes 12292
  81.2 20.8 %copy-start.15 = (f32[128]{0:T(128)}, f32[128]{0:T(128)S(1)}, u32[]{:S(2)}) copy-start(f32[128]{0:T(128)S(1)} %add_rsqrt_fusion) | copy-start | bytes 1540
  82.4 1.1 copy-start.17
  85.4 30.2 %all-to-all-start = ((s32[1,128,16]{2,0,1:T(1,128)}), s32[1,128,16]{2,0,1:T(1,128)S(1)}, u32[]{:S(2)}, u32[]{:S(2)}) async-start(s32[1,128,16]{2,0,1:T(1,128)} %copy.37), calls=%async_computation | async-start | bytes 131072 | tf_op jit(solution)/shard_map/all_to_all | solution.py:72
  103.3 0.8 copy-start.7
  117.0 6.4 %copy-start.12 = (s32[128,8]{0,1:T(8,128)S(1)}, s32[128,8]{0,1:T(8,128)}, u32[]{:S(2)}) copy-start(s32[128,8]{0,1:T(8,128)} %copy.36) | copy-start | bytes 12292
  117.1 6.6 %copy-start.14 = (s32[1024,1]{0,1:T(1,128)S(1)}, s32[1024,1]{0,1:T(1,128)}, u32[]{:S(2)}) copy-start(s32[1024,1]{0,1:T(1,128)} %mul.258) | copy-start | bytes 12292
  123.7 118.4 %copy-start.19 = (f32[128]{0:T(128)S(1)}, f32[128]{0:T(128)}, u32[]{:S(2)}) copy-start(f32[128]{0:T(128)} %get-tuple-element.8) | copy-start | bytes 1540
  123.7 128.9 %copy-start.13 = (s32[128,8]{0,1:T(8,128)S(1)}, s32[128,8]{0,1:T(8,128)}, u32[]{:S(2)}) copy-start(s32[128,8]{0,1:T(8,128)} %param.13) | copy-start | bytes 12292
  252.9 20.3 %copy-start.9 = (bf16[128,256]{1,0:T(8,128)(2,1)S(1)}, bf16[128,256]{1,0:T(8,128)(2,1)}, u32[]{:S(2)}) copy-start(bf16[128,256]{1,0:T(8,128)(2,1)} %get-tuple-element.9) | copy-start | bytes 196612
  259.4 26.5 %copy-start.18 = (f32[128]{0:T(128)S(1)}, f32[128]{0:T(128)}, u32[]{:S(2)}) copy-start(f32[128]{0:T(128)} %copy-done.17) | copy-start | bytes 1540
  259.4 65.0 %all-to-all-start.1 = ((bf16[128,16,256]{2,1,0:T(8,128)(2,1)}), bf16[128,16,256]{2,1,0:T(8,128)(2,1)}, u32[]{:S(2)}, u32[]{:S(2)}) async-start(bf16[128,16,256]{2,1,0:T(8,128)(2,1)} %bitcast.42), calls=%async_computation.2 | async-start | bytes 2097152 | tf_op jit(solution)/shard_map/all_to_all | solution.py:101
  271.5 82.6 %reduce-scatter.3.cloned.1.call-start = ((), (), s32[]{:S(2)}) async-start(), calls=%async_computation.5 | async-start | bytes 327680 | tf_op jit(solution)/shard_map/reduce_scatter | solution.py:51
  291.1 58.0 %copy-start.16 = (f32[128]{0:T(128)S(1)}, f32[128]{0:T(128)}, u32[]{:S(2)}) copy-start(f32[128]{0:T(128)} %copy-done.15) | copy-start | bytes 1540
  291.1 58.9 %copy-start.3 = (f32[128,1024]{1,0:T(8,128)S(1)}, f32[128,1024]{1,0:T(8,128)}, u32[]{:S(2)}) copy-start(f32[128,1024]{1,0:T(8,128)} %copy-done.2) | copy-start | bytes 1572868
  291.1 83.6 %reduce-scatter.5.cloned.1.call-start = ((), (), s32[]{:S(2)}) async-start(), calls=%async_computation.6 | async-start | bytes 327680 | tf_op jit(solution)/shard_map/reduce_scatter | solution.py:51
Sparse Core Ops, SparseCore 0:
  13.7 65.9 all-reduce.3
  84.8 146.7 all-gather.1
  291.2 27.8 reduce-scatter.2
  354.2 20.4 reduce-scatter.4
where the time goes:
time: 384 us; the launch traced here: 383 us
  waiting for transfers between devices  233 us (61%)
  blocking collectives  35.4 us (9%)
  other arithmetic  34.1 us (9%)
  starting transfers between devices  28.7 us (7%)
  local copies, waits for them, and re-layouts  22.1 us (6%)
  matrix products  14.9 us (4%)
  between operations  14.8 us (4%)
    all_gather x1, waiting for transfers between devices, shards(): every_emb = lax.all_gather(emb_pass, 'dp', axis=0, tiled=True)  108 us
    psum x1, waiting for transfers between devices, encode(): mixed_sum = lax.psum(partial_out, 'mp')  66 us
    all_to_all x1, waiting for transfers between devices, shards(): lax.all_to_all(outgoing_grad.reshape(owners, capacity, column_width), 'dp...  33.3 us
    all_gather x2, blocking collectives, decode(): lax.all_gather(grad_part.astype(jnp.bfloat16), 'mp', axis=1, tiled=True)  24.8 us
    reduce_scatter x2, waiting for transfers between devices, decode(): lax.psum_scatter(partial_in.astype(jnp.bfloat16), 'mp', scatter_dimension...  19.1 us
    all_to_all x1, starting transfers between devices, shards(): lax.all_to_all(served_rows, 'dp', split_axis=1, concat_axis=0, tiled=True)  16.5 us
    scatter-add x1, other arithmetic, shards(): gathered_back = jnp.zeros((row_count, column_width), jnp.float32).at[serv...  12.1 us
    all_to_all x1, starting transfers between devices, shards(): lax.all_to_all(outgoing_grad.reshape(owners, capacity, column_width), 'dp...  12 us
  transfers between devices with their start and end apart: 6, of which 5 were waited for; matrix products, arithmetic and copies ran while one was open for 11% of the time, Pallas kernels for 0%

commit v1 on v0

--- a/solution.py
+++ b/solution.py
@@ -62,23 +62,24 @@
     pre_pass, unit_pass, inv_pass = encode(passage_states, w_in, w_out)
     emb_pass = own_columns(unit_pass).astype(jnp.bfloat16)
     column_width = emb_pass.shape[1]
-    served = served_rows[0]
+    slots = owners * capacity
+    served = served_rows[0].reshape(-1)
+    served_pick = (served[:, None] == jnp.arange(row_count, dtype=jnp.int32)[None, :]).astype(jnp.bfloat16)
     flat_owner = neg_owner.reshape(-1)
     onehot = (flat_owner[:, None] == jnp.arange(owners, dtype=jnp.int32)[None, :]).astype(jnp.int32)
     before = jnp.cumsum(onehot, axis=0, dtype=jnp.int32) - onehot
     slot_index = jnp.sum(before * onehot, axis=1, dtype=jnp.int32)
-    slot_place = flat_owner * capacity + slot_index
-    every_emb = lax.all_gather(emb_pass, "dp", axis=0, tiled=True)
-    rows_for_me = lax.all_to_all(
-        served_rows, "dp", split_axis=1, concat_axis=0, tiled=True
-    ).reshape(owners * capacity)
-    neg_rows = jnp.take(rows_for_me, slot_place, axis=0)
-    neg_emb = jnp.take(every_emb, flat_owner * row_count + neg_rows, axis=0)
-    neg_emb = neg_emb.reshape(row_count, negatives, column_width)
+    slot_place = (flat_owner * capacity + slot_index).reshape(row_count, negatives)
+    outgoing_emb = jnp.dot(served_pick, emb_pass, preferred_element_type=jnp.float32).astype(jnp.bfloat16)
+    slot_emb = lax.all_to_all(
+        outgoing_emb.reshape(owners, capacity, column_width), "dp", split_axis=0, concat_axis=0, tiled=True
+    ).reshape(slots, column_width)
+    slot_hit = slot_place[:, :, None] == jnp.arange(slots, dtype=jnp.int32)[None, None, :]
     pre_query, unit_query, inv_query = encode(query_states, w_in, w_out)
     emb_query = own_columns(unit_query).astype(jnp.bfloat16)
     pos_part = jnp.einsum("qd,qd->q", emb_query, emb_pass, preferred_element_type=jnp.float32)
-    neg_part = jnp.einsum("qd,qnd->qn", emb_query, neg_emb, preferred_element_type=jnp.float32)
+    slot_part = lax.dot_general(emb_query, slot_emb, (((1,), (1,)), ((), ())), preferred_element_type=jnp.float32)
+    neg_part = jnp.sum(jnp.where(slot_hit, slot_part[:, None, :], 0.0), axis=2)
     pos_score, neg_score = lax.psum((pos_part, neg_part), "mp")
     exp_pos = jnp.exp(logit_scale * pos_score)
     exp_neg = neg_mask.astype(jnp.float32) * jnp.exp(logit_scale * neg_score)
@@ -87,29 +88,19 @@
     grad_pos = factor * (exp_pos / denominator - 1.0)
     grad_neg = factor * exp_neg / denominator[:, None]
     query_values = emb_query.astype(jnp.float32)
-    grad_query_emb = grad_pos[:, None] * emb_pass.astype(jnp.float32) + jnp.sum(
-        grad_neg[:, :, None] * neg_emb.astype(jnp.float32), axis=1
+    slot_grad = jnp.sum(jnp.where(slot_hit, grad_neg[:, :, None], 0.0), axis=1).astype(jnp.bfloat16)
+    grad_query_emb = grad_pos[:, None] * emb_pass.astype(jnp.float32) + jnp.dot(
+        slot_grad, slot_emb, preferred_element_type=jnp.float32
     )
-    slot_terms = (
-        (grad_neg[:, :, None] * query_values[:, None, :])
-        .astype(jnp.bfloat16)
-        .reshape(-1, column_width)
-    )
-    outgoing_grad = (
-        jnp.zeros((owners * capacity, column_width), jnp.bfloat16).at[slot_place].set(slot_terms)
-    )
+    outgoing_grad = lax.dot_general(
+        slot_grad, emb_query, (((0,), (0,)), ((), ())), preferred_element_type=jnp.float32
+    ).astype(jnp.bfloat16)
     returned = lax.all_to_all(
-        outgoing_grad.reshape(owners, capacity, column_width),
-        "dp",
-        split_axis=0,
-        concat_axis=0,
-        tiled=True,
-    )
+        outgoing_grad.reshape(owners, capacity, column_width), "dp", split_axis=0, concat_axis=0, tiled=True
+    ).reshape(slots, column_width)
     grad_query_states = decode(grad_query_emb, pre_query, unit_query, inv_query, w_in, w_out)
-    gathered_back = (
-        jnp.zeros((row_count, column_width), jnp.float32)
-        .at[served.reshape(-1)]
-        .add(returned.reshape(-1, column_width).astype(jnp.float32))
+    gathered_back = lax.dot_general(
+        served_pick, returned, (((0,), (0,)), ((), ())), preferred_element_type=jnp.float32
     )
     grad_pass_emb = grad_pos[:, None] * query_values + gathered_back
     grad_passage_states = decode(grad_pass_emb, pre_pass, unit_pass, inv_pass, w_in, w_out)

time: 384 us -> 283 us (0.74)
  the two profiles are of different devices: /device:TPU:4 before, /device:TPU:2 now
where the time goes in v1:
time: 283 us
  waiting for transfers between devices  167 us (59%)
  blocking collectives  35.1 us (12%)
  starting transfers between devices  26.6 us (9%)
  matrix products  20 us (7%)
  between operations  14.7 us (5%)
  other arithmetic  13 us (5%)
  local copies, waits for them, and re-layouts  5.84 us (2%)
    psum x1, waiting for transfers between devices, encode(): mixed_sum = lax.psum(partial_out, 'mp')  66 us
    all_to_all x1, waiting for transfers between devices, shards(): lax.all_to_all(outgoing_emb.reshape(owners, capacity, column_width), 'dp'...  48.6 us
    all_to_all x1, waiting for transfers between devices, shards(): lax.all_to_all(outgoing_grad.reshape(owners, capacity, column_width), 'dp...  32.9 us
    all_gather x2, blocking collectives, decode(): lax.all_gather(grad_part.astype(jnp.bfloat16), 'mp', axis=1, tiled=True)  25.2 us
    reduce_scatter x2, waiting for transfers between devices, decode(): lax.psum_scatter(partial_in.astype(jnp.bfloat16), 'mp', scatter_dimension...  19.8 us
    all_to_all x1, starting transfers between devices, shards(): lax.all_to_all(outgoing_emb.reshape(owners, capacity, column_width), 'dp'...  16.5 us
    all_to_all x1, starting transfers between devices, shards(): lax.all_to_all(outgoing_grad.reshape(owners, capacity, column_width), 'dp...  9.96 us
    psum x1, blocking collectives, shards(): pos_score, neg_score = lax.psum((pos_part, neg_part), 'mp')  9.87 us
  transfers between devices with their start and end apart: 5, of which 4 were waited for; matrix products, arithmetic and copies ran while one was open for 6% of the time, Pallas kernels for 0%

profile of v1, /device:TPU:2, one launch (start us, length us, event | category | flops | bytes accessed | tf_op | source)
XLA Modules:
  0.0 282.5 jit_solution(1490627160886354186)
XLA Ops:
  7.2 2.3 fusion.56
  10.2 0.8 copy-done.7
  11.0 1.3 fusion.29
  12.3 1.3 fusion.28
  13.8 66.0 %all-reduce.4.cloned.1.call-done = (f32[128,1024]{1,0:T(8,128)}, f32[128,1024]{1,0:T(8,128)}) async-done(((f32[128,1024]{1,0:T(8,128)}, f32[128,1024]{1,0:T(8,128)}), (f32[128,1024]{1,0:T(8,128)}, f32[128,1024]{1,0:T(8,128)})) %all-reduce.4.cloned.1.call-update) | async-done | bytes 1048592 | tf_op jit(solution)/shard_map/psum | solution.py:32
  79.7 1.5 multiply_reduce_fusion
  81.2 1.1 fusion.27
  82.5 0.6 copy-done.2
  83.3 0.7 copy-done.4
  84.0 1.5 convolution_convert_fusion.1
  85.5 16.5 %all-to-all-start = ((bf16[128,16,256]{2,1,0:T(8,128)(2,1)}), bf16[128,16,256]{2,1,0:T(8,128)(2,1)S(1)}, u32[]{:S(2)}, u32[]{:S(2)}) async-start(bf16[128,16,256]{2,1,0:T(8,128)(2,1)} %bitcast.34), calls=%async_computation | async-start | bytes 2097152 | tf_op jit(solution)/shard_map/all_to_all | solution.py:74
  103.2 0.8 copy-done.14
  104.1 1.1 broadcast_add_fusion
  105.9 48.6 %all-to-all-done = bf16[128,16,256]{2,1,0:T(8,128)(2,1)S(1)} async-done(((bf16[128,16,256]{2,1,0:T(8,128)(2,1)}), bf16[128,16,256]{2,1,0:T(8,128)(2,1)S(1)}, u32[]{:S(2)}, u32[]{:S(2)}) %all-to-all-start) | async-done | bytes 1048608 | tf_op jit(solution)/shard_map/all_to_all | solution.py:74
  155.0 1.1 select_reduce_fusion.1
  156.2 9.9 %all-reduce = (f32[128,8]{0,1:T(8,128)S(1)}, f32[128]{0:T(128)S(1)}) all-reduce(f32[128,8]{0,1:T(8,128)S(1)} %copy.35, f32[128]{0:T(128)S(1)} %get-tuple-element.6), channel_id=1, replica_groups=mesh['dp'=128,'mp'=4] {'mp'}, use_global_device_ids=true, to_apply=%region_9.10 | all-reduce | flops 1152 | bytes 9216 | tf_op jit(solution)/shard_map/psum | solution.py:83
  166.2 2.8 select_reduce_fusion
  169.1 0.8 copy-done.6
  169.8 1.5 convolution_convert_fusion
  171.3 10.0 %all-to-all-start.1 = ((bf16[128,16,256]{2,1,0:T(8,128)(2,1)}), bf16[128,16,256]{2,1,0:T(8,128)(2,1)}, u32[]{:S(2)}, u32[]{:S(2)}) async-start(bf16[128,16,256]{2,1,0:T(8,128)(2,1)} %bitcast.35), calls=%async_computation.2 | async-start | bytes 2097152 | tf_op jit(solution)/shard_map/all_to_all | solution.py:98
  181.4 1.4 fusion.2
  182.8 12.8 %all_gather.6 = bf16[128,1024]{1,0:T(8,128)(2,1)S(1)} all-gather(bf16[128,256]{1,0:T(8,128)(2,1)S(1)} %fusion.2), channel_id=1, replica_groups=mesh['dp'=128,'mp'=4] {'mp'}, dimensions={1}, use_global_device_ids=true | all-gather | bytes 327680 | tf_op jit(solution)/shard_map/all_gather | solution.py:39
  195.9 0.8 copy-done.11
  196.7 3.8 %convolution_convert_fusion.3 = bf16[128,1024]{1,0:T(8,128)(2,1)} fusion(bf16[1024,1024]{1,0:T(8,128)(2,1)} %param.10, bf16[1024,1024]{1,0:T(8,128)(2,1)S(1)} %copy-done, f32[128,1024]{1,0:T(8,128)S(1)} %copy-done.10, f32[128,1024]{1,0:T(8,128)S(1)} %fusion.5), kind=kOutput, calls=%fused_computation.8 | convolution fusion | flops 538443776 | bytes 5505024 | tf_op jit(solution)/shard_map/dot_general | solution.py:50
  200.6 32.9 %all-to-all-done.1 = bf16[128,16,256]{2,1,0:T(8,128)(2,1)} async-done(((bf16[128,16,256]{2,1,0:T(8,128)(2,1)}), bf16[128,16,256]{2,1,0:T(8,128)(2,1)}, u32[]{:S(2)}, u32[]{:S(2)}) %all-to-all-start.1) | async-done | bytes 1048608 | tf_op jit(solution)/shard_map/all_to_all | solution.py:98
  233.5 2.0 fusion.3
  235.5 12.4 %all_gather.7 = bf16[128,1024]{1,0:T(8,128)(2,1)S(1)} all-gather(bf16[128,256]{1,0:T(8,128)(2,1)S(1)} %fusion.3), channel_id=1, replica_groups=mesh['dp'=128,'mp'=4] {'mp'}, dimensions={1}, use_global_device_ids=true | all-gather | bytes 327680 | tf_op jit(solution)/shard_map/all_gather | solution.py:39
  248.1 1.0 fusion.7
  249.1 4.0 %convolution_convert_fusion.2 = bf16[128,1024]{1,0:T(8,128)(2,1)} fusion(bf16[1024,1024]{1,0:T(8,128)(2,1)} %param.10, bf16[1024,1024]{1,0:T(8,128)(2,1)S(1)} %copy-done, f32[128,1024]{1,0:T(8,128)S(1)} %copy-done.8, f32[128,1024]{1,0:T(8,128)} %fusion.7), kind=kOutput, calls=%fused_computation.7 | convolution fusion | flops 538443776 | bytes 5505024 | tf_op jit(solution)/shard_map/dot_general | solution.py:50
  253.1 1.6 add_convert_fusion.1
  254.7 19.8 %reduce-scatter.5.cloned.1.call-done = bf16[128,256]{1,0:T(8,128)(2,1)} async-done(((bf16[128,1024]{1,0:T(8,128)(2,1)}), bf16[128,256]{1,0:T(8,128)(2,1)}) %reduce-scatter.5.cloned.1.call-update) | async-done | bytes 65552 | tf_op jit(solution)/shard_map/reduce_scatter | solution.py:51
  274.5 1.5 add_convert_fusion
  (69 shorter events, 3.7 us)
Async XLA Ops:
  7.2 3.8 %copy-start = (bf16[1024,1024]{1,0:T(8,128)(2,1)S(1)}, bf16[1024,1024]{1,0:T(8,128)(2,1)}, u32[]{:S(2)}) copy-start(bf16[1024,1024]{1,0:T(8,128)(2,1)} %param.11) | copy-start | bytes 6291460
  7.2 2.3 copy-start.12
  7.2 72.5 %all-reduce.4.cloned.1.call-start = ((), (), s32[]{:S(2)}) async-start(), calls=%async_computation.6 | async-start | bytes 2097152 | tf_op jit(solution)/shard_map/psum | solution.py:32
  7.2 2.5 copy-start.1
  9.7 2.5 copy-start.9
  10.2 0.8 copy-start.7
  12.3 1.3 copy-start.18
  12.3 67.5 %copy-start.13 = (bf16[128,1024]{1,0:T(8,128)(2,1)S(1)}, bf16[128,1024]{1,0:T(8,128)(2,1)}, u32[]{:S(2)}) copy-start(bf16[128,1024]{1,0:T(8,128)(2,1)} %param.8) | copy-start | bytes 786436
  79.7 2.7 copy-start.15
  82.4 0.8 copy-start.2
  82.4 19.6 %copy-start.16 = (s32[128,8]{0,1:T(8,128)S(1)}, s32[128,8]{0,1:T(8,128)}, u32[]{:S(2)}) copy-start(s32[128,8]{0,1:T(8,128)} %param.12) | copy-start | bytes 12292
  83.2 0.8 copy-start.4
  85.5 69.1 %all-to-all-start = ((bf16[128,16,256]{2,1,0:T(8,128)(2,1)}), bf16[128,16,256]{2,1,0:T(8,128)(2,1)S(1)}, u32[]{:S(2)}, u32[]{:S(2)}) async-start(bf16[128,16,256]{2,1,0:T(8,128)(2,1)} %bitcast.34), calls=%async_computation | async-start | bytes 2097152 | tf_op jit(solution)/shard_map/all_to_all | solution.py:74
  103.2 0.8 copy-start.14
  105.3 60.8 %copy-start.17 = (s32[128,8]{0,1:T(8,128)S(1)}, s32[128,8]{0,1:T(8,128)}, u32[]{:S(2)}) copy-start(s32[128,8]{0,1:T(8,128)} %param.13) | copy-start | bytes 12292
  169.0 0.8 copy-start.6
  171.3 62.2 %all-to-all-start.1 = ((bf16[128,16,256]{2,1,0:T(8,128)(2,1)}), bf16[128,16,256]{2,1,0:T(8,128)(2,1)}, u32[]{:S(2)}, u32[]{:S(2)}) async-start(bf16[128,16,256]{2,1,0:T(8,128)(2,1)} %bitcast.35), calls=%async_computation.2 | async-start | bytes 2097152 | tf_op jit(solution)/shard_map/all_to_all | solution.py:98
  181.3 71.8 %reduce-scatter.3.cloned.1.call-start = ((), (), s32[]{:S(2)}) async-start(), calls=%async_computation.4 | async-start | bytes 327680 | tf_op jit(solution)/shard_map/reduce_scatter | solution.py:51
  181.4 14.2 %copy-start.5 = (f32[128,1024]{1,0:T(8,128)S(1)}, f32[128,1024]{1,0:T(8,128)}, u32[]{:S(2)}) copy-start(f32[128,1024]{1,0:T(8,128)} %copy-done.4) | copy-start | bytes 1572868
  182.8 13.9 %copy-start.10 = (f32[128,1024]{1,0:T(8,128)S(1)}, f32[128,1024]{1,0:T(8,128)}, u32[]{:S(2)}) copy-start(f32[128,1024]{1,0:T(8,128)} %copy-done.9) | copy-start | bytes 1572868
  195.9 0.8 copy-start.11
  200.5 47.4 %copy-start.3 = (f32[128,1024]{1,0:T(8,128)S(1)}, f32[128,1024]{1,0:T(8,128)}, u32[]{:S(2)}) copy-start(f32[128,1024]{1,0:T(8,128)} %copy-done.2) | copy-start | bytes 1572868
  200.5 48.5 %copy-start.8 = (f32[128,1024]{1,0:T(8,128)S(1)}, f32[128,1024]{1,0:T(8,128)}, u32[]{:S(2)}) copy-start(f32[128,1024]{1,0:T(8,128)} %copy-done.7) | copy-start | bytes 1572868
  200.6 73.9 %reduce-scatter.5.cloned.1.call-start = ((), (), s32[]{:S(2)}) async-start(), calls=%async_computation.5 | async-start | bytes 327680 | tf_op jit(solution)/shard_map/reduce_scatter | solution.py:51
Sparse Core Ops, SparseCore 0:
  13.7 65.9 all-reduce.3
  200.7 27.8 reduce-scatter.2
  253.2 21.1 reduce-scatter.4

commit v2 on v1

v2 whole, which is shorter than its diff:
```python
import functools
import jax
import jax.numpy as jnp
from jax import lax
from jax.experimental import pallas as pl
from jax.experimental.pallas import tpu as pltpu
from jax.sharding import PartitionSpec as P

logit_scale = 50.0
norm_eps = 1e-06
root_half = 0.7071067811865476
inv_root_two_pi = 0.3989422804014327


def gelu_value(values):
    return 0.5 * values * (1.0 + lax.erf(values * root_half))


def gelu_slope(values):
    return (
        0.5 * (1.0 + lax.erf(values * root_half))
        + values * jnp.exp(-0.5 * values * values) * inv_root_two_pi
    )


def own_columns(values):
    column_width = values.shape[1] // lax.axis_size("mp")
    return lax.dynamic_slice_in_dim(values, lax.axis_index("mp") * column_width, column_width, 1)


def greet(ways):
    me = lax.axis_index("mp")
    barrier = pltpu.get_barrier_semaphore()
    for step in range(1, ways):
        pl.semaphore_signal(
            barrier, inc=1, device_id={"mp": lax.rem(me + step, ways)}, device_id_type=pl.DeviceIdType.MESH
        )
    pl.semaphore_wait(barrier, ways - 1)
    return me


def remote(source, target, send_sem, recv_sem, peer):
    return pltpu.make_async_remote_copy(
        src_ref=source,
        dst_ref=target,
        send_sem=send_sem,
        recv_sem=recv_sem,
        device_id={"mp": peer},
        device_id_type=pl.DeviceIdType.MESH,
    )


def block_of(ref, place, width):
    return ref.at[:, pl.ds(pl.multiple_of(place * width, 128), width)]


def scatter_kernel(ways, part_ref, out_ref, landed, send_sem, recv_sem):
    width = out_ref.shape[1]
    me = greet(ways)
    copies = []
    for step in range(1, ways):
        peer = lax.rem(me + step, ways)
        copy = remote(
            block_of(part_ref, peer, width),
            landed.at[step - 1],
            send_sem.at[step - 1],
            recv_sem.at[step - 1],
            peer,
        )
        copy.start()
        copies.append(copy)
    for copy in copies:
        copy.wait()
    own = part_ref[:, pl.ds(pl.multiple_of(me * width, 128), width)]
    total = own.astype(jnp.float32)
    for step in range(1, ways):
        total = total + landed[step - 1].astype(jnp.float32)
    out_ref[...] = total


def gather_kernel(ways, own_ref, out_ref, send_sem, recv_sem):
    width = own_ref.shape[1]
    me = greet(ways)
    copies = []
    for step in range(1, ways):
        copy = remote(
            own_ref,
            block_of(out_ref, me, width),
            send_sem.at[step - 1],
            recv_sem.at[step - 1],
            lax.rem(me + step, ways),
        )
        copy.start()
        copies.append(copy)
    out_ref[:, pl.ds(pl.multiple_of(me * width, 128), width)] = own_ref[...]
    for copy in copies:
        copy.wait()


def gather_sum_kernel(ways, own_ref, term_ref, out_ref, sum_ref, landed, send_sem, recv_sem, term_send, term_recv):
    width = own_ref.shape[1]
    me = greet(ways)
    copies = []
    for step in range(1, ways):
        peer = lax.rem(me + step, ways)
        term_copy = remote(
            term_ref, landed.at[step - 1], term_send.at[step - 1], term_recv.at[step - 1], peer
        )
        copy = remote(
            own_ref, block_of(out_ref, me, width), send_sem.at[step - 1], recv_sem.at[step - 1], peer
        )
        copy.start()
        term_copy.start()
        copies += [copy, term_copy]
    out_ref[:, pl.ds(pl.multiple_of(me * width, 128), width)] = own_ref[...]
    for copy in copies:
        copy.wait()
    total = term_ref[...]
    for step in range(1, ways):
        total = total + landed[step - 1]
    sum_ref[...] = total


def sum_kernel(ways, term_ref, sum_ref, landed, send_sem, recv_sem):
    me = greet(ways)
    copies = []
    for step in range(1, ways):
        copy = remote(
            term_ref,
            landed.at[step - 1],
            send_sem.at[step - 1],
            recv_sem.at[step - 1],
            lax.rem(me + step, ways),
        )
        copy.start()
        copies.append(copy)
    for copy in copies:
        copy.wait()
    total = term_ref[...]
    for step in range(1, ways):
        total = total + landed[step - 1]
    sum_ref[...] = total


def in_vmem(count):
    return [pl.BlockSpec(memory_space=pltpu.VMEM)] * count


def params(number):
    return pltpu.CompilerParams(collective_id=number, has_side_effects=True, vmem_limit_bytes=16 << 20)


def sems(ways):
    return [pltpu.SemaphoreType.DMA((ways - 1,)), pltpu.SemaphoreType.DMA((ways - 1,))]


def mp_scatter(part, number):
    ways = lax.axis_size("mp")
    rows, width = part.shape[0], part.shape[1] // ways
    return pl.pallas_call(
        functools.partial(scatter_kernel, ways),
        out_shape=jax.ShapeDtypeStruct((rows, width), jnp.float32),
        in_specs=in_vmem(1),
        out_specs=pl.BlockSpec(memory_space=pltpu.VMEM),
        scratch_shapes=[pltpu.VMEM((ways - 1, rows, width), part.dtype)] + sems(ways),
        compiler_params=params(number),
        cost_estimate=pl.CostEstimate(flops=rows * width * 4, bytes_accessed=part.size * 4, transcendentals=0),
        name="mp_scatter",
    )(part)


def mp_gather(own, number):
    ways = lax.axis_size("mp")
    rows, width = own.shape
    return pl.pallas_call(
        functools.partial(gather_kernel, ways),
        out_shape=jax.ShapeDtypeStruct((rows, ways * width), own.dtype),
        in_specs=in_vmem(1),
        out_specs=pl.BlockSpec(memory_space=pltpu.VMEM),
        scratch_shapes=sems(ways),
        compiler_params=params(number),
        cost_estimate=pl.CostEstimate(flops=0, bytes_accessed=own.size * 10, transcendentals=0),
        name="mp_gather",
    )(own)


def mp_gather_sum(own, term, number):
    ways = lax.axis_size("mp")
    rows, width = own.shape
    return pl.pallas_call(
        functools.partial(gather_sum_kernel, ways),
        out_shape=(
            jax.ShapeDtypeStruct((rows, ways * width), own.dtype),
            jax.ShapeDtypeStruct(term.shape, term.dtype),
        ),
        in_specs=in_vmem(2),
        out_specs=tuple(in_vmem(2)),
        scratch_shapes=[pltpu.VMEM((ways - 1,) + term.shape, term.dtype)] + sems(ways) + sems(ways),
        compiler_params=params(number),
        cost_estimate=pl.CostEstimate(flops=0, bytes_accessed=own.size * 10, transcendentals=0),
        name="mp_gather_sum",
    )(own, term)


def mp_sum(term, number):
    ways = lax.axis_size("mp")
    return pl.pallas_call(
        functools.partial(sum_kernel, ways),
        out_shape=jax.ShapeDtypeStruct(term.shape, term.dtype),
        in_specs=in_vmem(1),
        out_specs=pl.BlockSpec(memory_space=pltpu.VMEM),
        scratch_shapes=[pltpu.VMEM((ways - 1,) + term.shape, term.dtype)] + sems(ways),
        compiler_params=params(number),
        cost_estimate=pl.CostEstimate(flops=0, bytes_accessed=term.size * 20, transcendentals=0),
        name="mp_sum",
    )(term)


def decode(grad_own, pre_act, out_own, out_full, inv_norm, w_in, w_out, number):
    inv = inv_norm[:, None]
    unit_own = out_own * inv
    dot_part = jnp.sum(unit_own * grad_own, axis=1)
    grad_full, dots = mp_gather_sum(
        grad_own.astype(jnp.bfloat16), jnp.broadcast_to(dot_part[None, :], (8, dot_part.shape[0])), number
    )
    dot_all = dots[0][:, None]
    grad_out = inv * (grad_full.astype(jnp.float32) - out_full.astype(jnp.float32) * (inv * dot_all))
    grad_out_own = inv * (grad_own - unit_own * dot_all)
    contract = (((1,), (1,)), ((), ()))
    grad_hidden = lax.dot_general(
        grad_out.astype(jnp.bfloat16), w_out, contract, preferred_element_type=jnp.float32
    )
    grad_pre = (grad_hidden * gelu_slope(pre_act)).astype(jnp.bfloat16)
    partial_in = lax.dot_general(grad_pre, w_in, contract, preferred_element_type=jnp.float32)
    summed = mp_scatter(partial_in.astype(jnp.bfloat16), number + 1)
    return (summed + grad_out_own).astype(jnp.bfloat16)


def shards(query_states, passage_states, w_in, w_out, neg_owner, neg_mask, served_rows, loss_scale):
    owners = lax.axis_size("dp")
    row_count = query_states.shape[0]
    capacity = served_rows.shape[2]
    slots = owners * capacity
    states = jnp.concatenate([passage_states, query_states], axis=0)
    pre_act = jnp.dot(states, w_in, preferred_element_type=jnp.float32)
    hidden = gelu_value(pre_act).astype(jnp.bfloat16)
    partial_out = jnp.dot(hidden, w_out, preferred_element_type=jnp.float32).astype(jnp.bfloat16)
    out_own = own_columns(states).astype(jnp.float32) + mp_scatter(partial_out, 0)
    out_pass, out_query = out_own[:row_count], out_own[row_count:]
    out_half = out_own.astype(jnp.bfloat16)
    half_pass, half_query = out_half[:row_count], out_half[row_count:]
    column_width = half_pass.shape[1]

    served = served_rows[0].reshape(-1)
    served_pick = (served[:, None] == jnp.arange(row_count, dtype=jnp.int32)[None, :]).astype(jnp.bfloat16)
    flat_owner = neg_owner.reshape(-1)
    onehot = (flat_owner[:, None] == jnp.arange(owners, dtype=jnp.int32)[None, :]).astype(jnp.int32)
    before = jnp.cumsum(onehot, axis=0, dtype=jnp.int32) - onehot
    slot_index = jnp.sum(before * onehot, axis=1, dtype=jnp.int32)
    slot_place = (flat_owner * capacity + slot_index).reshape(neg_owner.shape).T
    outgoing_rows = jnp.dot(served_pick, half_pass, preferred_element_type=jnp.float32).astype(jnp.bfloat16)
    slot_rows = lax.all_to_all(
        outgoing_rows.reshape(owners, capacity, column_width), "dp", split_axis=0, concat_axis=0, tiled=True
    ).reshape(slots, column_width)
    out_full = mp_gather(out_half, 1)
    slot_hit = slot_place[:, :, None] == jnp.arange(slots, dtype=jnp.int32)[None, None, :]

    slot_part = lax.dot_general(half_query, slot_rows, (((1,), (1,)), ((), ())), preferred_element_type=jnp.float32)
    slot_wide = slot_rows.astype(jnp.float32)
    slot_square = jnp.sum(slot_wide * slot_wide, axis=1)
    neg_part = jnp.sum(jnp.where(slot_hit, slot_part[None, :, :], 0.0), axis=2)
    neg_square = jnp.sum(jnp.where(slot_hit, slot_square[None, None, :], 0.0), axis=2)
    pos_part = jnp.sum(half_query.astype(jnp.float32) * half_pass.astype(jnp.float32), axis=1)
    squares = jnp.sum(out_own * out_own, axis=1).reshape(2, row_count)
    extra = jnp.concatenate([pos_part[None, :], squares, jnp.zeros((5, row_count), jnp.float32)], axis=0)
    sums = mp_sum(jnp.concatenate([neg_part, neg_square, extra], axis=0), 2)
    negatives = neg_owner.shape[1]
    inv_neg = lax.rsqrt(sums[negatives : 2 * negatives] + norm_eps)
    inv_pass = lax.rsqrt(sums[2 * negatives + 1] + norm_eps)
    inv_query = lax.rsqrt(sums[2 * negatives + 2] + norm_eps)
    pos_score = sums[2 * negatives] * inv_query * inv_pass
    neg_score = sums[:negatives] * inv_query[None, :] * inv_neg
    exp_pos = jnp.exp(logit_scale * pos_score)
    exp_neg = neg_mask.T.astype(jnp.float32) * jnp.exp(logit_scale * neg_score)
    denominator = exp_pos + jnp.sum(exp_neg, axis=0)
    factor = loss_scale * logit_scale
    grad_pos = factor * (exp_pos / denominator - 1.0)
    grad_neg = factor * exp_neg / denominator[None, :]

    slot_grad = jnp.sum(jnp.where(slot_hit, (grad_neg * inv_query[None, :])[:, :, None], 0.0), axis=0)
    outgoing_grad = lax.dot_general(
        slot_grad.astype(jnp.bfloat16), half_query, (((0,), (0,)), ((), ())), preferred_element_type=jnp.float32
    ).astype(jnp.bfloat16)
    returned = lax.all_to_all(
        outgoing_grad.reshape(owners, capacity, column_width), "dp", split_axis=0, concat_axis=0, tiled=True
    ).reshape(slots, column_width)
    slot_weight = jnp.sum(jnp.where(slot_hit, (grad_neg * inv_neg)[:, :, None], 0.0), axis=0)
    grad_query_emb = (grad_pos * inv_pass)[:, None] * out_pass + jnp.dot(
        slot_weight.astype(jnp.bfloat16), slot_rows, preferred_element_type=jnp.float32
    )
    grad_query_states = decode(
        grad_query_emb, pre_act[row_count:], out_query, out_full[row_count:], inv_query, w_in, w_out, 3
    )
    returned, grad_query_states = lax.optimization_barrier((returned, grad_query_states))
    gathered_back = lax.dot_general(
        served_pick, returned, (((0,), (0,)), ((), ())), preferred_element_type=jnp.float32
    )
    grad_pass_emb = (grad_pos * inv_query)[:, None] * out_query + gathered_back
    grad_passage_states = decode(
        grad_pass_emb, pre_act[:row_count], out_pass, out_full[:row_count], inv_pass, w_in, w_out, 5
    )
    return (grad_query_states, grad_passage_states)


def solution(mesh):
    in_specs = (
        P("dp", None),
        P("dp", None),
        P(None, "mp"),
        P("mp", None),
        P("dp", None),
        P("dp", None),
        P("dp", None, None),
        P(),
    )
    out_specs = (P("dp", "mp"), P("dp", "mp"))
    return jax.shard_map(shards, mesh=mesh, in_specs=in_specs, out_specs=out_specs, check_vma=False)
```

time: 283 us -> 200 us (0.71)
  the two profiles are of different devices: /device:TPU:2 before, /device:TPU:32 now
where the time goes in v2:
time: 200 us; the launch traced here: 199 us
  waiting for transfers between devices  66.1 us (33%)
  Pallas kernels  59.3 us (30%)
  starting transfers between devices  26.3 us (13%)
  other arithmetic  16.6 us (8%)
  matrix products  16.2 us (8%)
  local copies, waits for them, and re-layouts  13.1 us (7%)
    all_to_all x1, waiting for transfers between devices, shards(): lax.all_to_all(outgoing_rows.reshape(owners, capacity, column_width), 'dp...  44.9 us
    pallas_call x3, Pallas kernels, mp_scatter(): pl.pallas_call(functools.partial(scatter_kernel, ways), out_shape=jax.Sha...  26.3 us
    all_to_all x1, waiting for transfers between devices, shards(): lax.all_to_all(outgoing_grad.reshape(owners, capacity, column_width), 'dp...  21.2 us
    all_to_all x1, starting transfers between devices, shards(): lax.all_to_all(outgoing_rows.reshape(owners, capacity, column_width), 'dp...  19 us
    pallas_call x2, Pallas kernels, mp_gather_sum(): pl.pallas_call(functools.partial(gather_sum_kernel, ways), out_shape=(jax...  16.3 us
    pallas_call x1, Pallas kernels, mp_gather(): pl.pallas_call(functools.partial(gather_kernel, ways), out_shape=jax.Shap...  10.6 us
    all_to_all x1, starting transfers between devices, shards(): lax.all_to_all(outgoing_grad.reshape(owners, capacity, column_width), 'dp...  7.29 us
    dot_general x2, matrix products, decode(): lax.dot_general(grad_pre, w_in, contract, preferred_element_type=jnp.floa...  6.51 us
  transfers between devices with their start and end apart: 2, of which 2 were waited for; matrix products, arithmetic and copies ran while one was open for 8% of the time, Pallas kernels for 13%

profile of v2, /device:TPU:32, one launch (start us, length us, event | category | flops | bytes accessed | tf_op | source)
XLA Modules:
  0.0 199.2 jit_solution(8508754032418195676)
XLA Ops:
  0.6 0.9 copy.31
  1.6 1.0 constant_dynamic-update-slice_fusion.1
  2.6 1.1 constant_dynamic-update-slice_fusion
  5.2 1.0 copy-done.4
  7.0 11.4 %mp_scatter.3 = f32[256,256]{1,0:T(8,128)S(1)} custom-call(bf16[256,1024]{1,0:T(8,128)(2,1)S(1)} %convolution_convert_fusion.2.part_ref), custom_call_target="tpu_custom_call" | custom-call | flops 262144 | bytes 1048576 | tf_op jit(solution)/shard_map/mp_scatter/pallas_call | solution.py:160
  18.4 1.6 multiply_reduce_fusion.1
  20.0 1.5 convolution_convert_fusion.1
  21.5 19.0 %all-to-all-start = ((bf16[128,16,256]{2,1,0:T(8,128)(2,1)}), bf16[128,16,256]{2,1,0:T(8,128)(2,1)S(1)}, u32[]{:S(2)}, u32[]{:S(2)}) async-start(bf16[128,16,256]{2,1,0:T(8,128)(2,1)} %bitcast.72), calls=%async_computation | async-start | bytes 2097152 | tf_op jit(solution)/shard_map/all_to_all | solution.py:262
  41.3 0.9 eq.57
  42.2 0.9 eq.53
  44.5 1.0 fusion.31
  46.4 1.1 broadcast_add_fusion
  50.9 44.9 %all-to-all-done = bf16[128,16,256]{2,1,0:T(8,128)(2,1)S(1)} async-done(((bf16[128,16,256]{2,1,0:T(8,128)(2,1)}), bf16[128,16,256]{2,1,0:T(8,128)(2,1)S(1)}, u32[]{:S(2)}, u32[]{:S(2)}) %all-to-all-start) | async-done | bytes 1048608 | tf_op jit(solution)/shard_map/all_to_all | solution.py:262
  95.8 1.0 multiply_reduce_fusion
  96.8 0.9 broadcast_in_dim.75
  98.2 3.4 %select_reduce_fusion.2 = (f32[8,128]{1,0:T(8,128)S(1)}, f32[8,128]{1,0:T(8,128)}) fusion(f32[2048]{0:T(1024)S(1)} %broadcast_in_dim.75, s32[8,128]{1,0:T(8,128)S(1)} %add_bitcast_fusion, f32[128,2048]{1,0:T(8,128)S(1)} %fusion.58), kind=kLoop, calls=%fused_computation.2 | loop fusion | flops 10483712 | bytes 1069056 | tf_op jit(solution)/shard_map/reduce_sum | solution.py:272
  101.7 1.4 concatenate.7.term_ref
  103.0 6.1 %mp_sum.1 = f32[24,128]{1,0:T(8,128)S(1)} custom-call(f32[24,128]{1,0:T(8,128)S(1)} %concatenate.7.term_ref), custom_call_target="tpu_custom_call" | custom-call | bytes 61440 | tf_op jit(solution)/shard_map/mp_sum/pallas_call | solution.py:207
  110.5 2.4 %select_reduce_fusion = (bf16[128,2048]{1,0:T(8,128)(2,1)S(1)}, bf16[128,2048]{1,0:T(8,128)(2,1)S(1)}) fusion(f32[8,128]{1,0:T(8,128)S(1)} %get-tuple-element.31, s32[8,128]{1,0:T(8,128)S(1)} %add_bitcast_fusion, f32[8,128]{1,0:T(8,128)S(1)} %get-tuple-element.30), kind=kLoop, calls=%fused_computation | loop fusion | flops 9961472 | bytes 1060864 | tf_op jit(solution)/shard_map/reduce_sum | solution.py:297
  112.8 1.4 convolution_convert_fusion
  114.3 7.3 %all-to-all-start.1 = ((bf16[128,16,256]{2,1,0:T(8,128)(2,1)}), bf16[128,16,256]{2,1,0:T(8,128)(2,1)}, u32[]{:S(2)}, u32[]{:S(2)}) async-start(bf16[128,16,256]{2,1,0:T(8,128)(2,1)} %bitcast.12), calls=%async_computation.1 | async-start | bytes 2097152 | tf_op jit(solution)/shard_map/all_to_all | solution.py:294
  121.6 10.6 %mp_gather.1 = bf16[256,1024]{1,0:T(8,128)(2,1)S(1)} custom-call(bf16[256,256]{1,0:T(8,128)(2,1)S(1)} %convert_element_type.97.own_ref), custom_call_target="tpu_custom_call" | custom-call | bytes 655360 | tf_op jit(solution)/shard_map/mp_gather/pallas_call | solution.py:175
  132.9 2.2 %multiply_reduce_fusion.3 = (f32[128]{0:T(128)S(1)}, bf16[128,256]{1,0:T(8,128)(2,1)S(1)}, f32[128,256]{1,0:T(8,128)}) fusion(f32[256,256]{1,0:T(8,128)S(1)} %get-tuple-element.23, f32[128]{0:T(128)S(1)} %copy-done.10, bf16[128,2048]{1,0:T(8,128)(2,1)S(1)} %get-tuple-element.14, bf16[2048,256]{1,0:T(8,128)(2,1)} %bitcast.71, f32[128]{0:T(128)S(1)} %bitcast_multiply_fusion.3), kind=kOutput, calls=%fused_computation.78 | convolution fusion | flops 134414208 | bytes 2033152 | tf_op jit(solution)/shard_map/dot_general | solution.py:298
  135.1 7.9 %mp_gather_sum.2 = (bf16[128,1024]{1,0:T(8,128)(2,1)S(1)}, f32[8,128]{1,0:T(8,128)S(1)}) custom-call(bf16[128,256]{1,0:T(8,128)(2,1)S(1)} %get-tuple-element.27.own_ref, f32[8,128]{1,0:T(8,128)S(1)} %broadcast_in_dim.81.term_ref), custom_call_target="tpu_custom_call" | custom-call | bytes 327680 | tf_op jit(solution)/shard_map/mp_gather_sum/pallas_call | solution.py:190
  143.1 3.2 %convolution_convert_fusion.4.part_ref = bf16[128,1024]{1,0:T(8,128)(2,1)S(1)} fusion(bf16[1024,1024]{1,0:T(8,128)(2,1)S(1)} %copy-done, bf16[1024,1024]{1,0:T(8,128)(2,1)} %param.11, f32[256,1024]{1,0:T(8,128)} %copy-done.4, bf16[128,1024]{1,0:T(8,128)(2,1)S(1)} %get-tuple-element.8, f32[128]{0:T(128)S(1)} %bitcast_multiply_fusion.5, ...), kind=kOutput, calls=%fused_computation.12 | convolution fusion | flops 539099136 | bytes 5506048 | tf_op jit(solution)/shard_map/dot_general | solution.py:234
  146.3 7.3 %mp_scatter.4 = f32[128,256]{1,0:T(8,128)S(1)} custom-call(bf16[128,1024]{1,0:T(8,128)(2,1)S(1)} %convolution_convert_fusion.4.part_ref), custom_call_target="tpu_custom_call" | custom-call | flops 131072 | bytes 524288 | tf_op jit(solution)/shard_map/mp_scatter/pallas_call | solution.py:160
  153.6 1.6 add_convert_fusion.1
  155.3 21.2 %all-to-all-done.1 = bf16[128,16,256]{2,1,0:T(8,128)(2,1)} async-done(((bf16[128,16,256]{2,1,0:T(8,128)(2,1)}), bf16[128,16,256]{2,1,0:T(8,128)(2,1)}, u32[]{:S(2)}, u32[]{:S(2)}) %all-to-all-start.1) | async-done | bytes 1048608 | tf_op jit(solution)/shard_map/all_to_all | solution.py:294
  176.5 2.6 %multiply_reduce_fusion.2 = (f32[128]{0:T(128)S(1)}, bf16[128,256]{1,0:T(8,128)(2,1)S(1)}, f32[128,256]{1,0:T(8,128)}) fusion(f32[256,256]{1,0:T(8,128)S(1)} %get-tuple-element.23, f32[128]{0:T(128)S(1)} %copy-done.12, bf16[2048,256]{1,0:T(8,128)(2,1)} %bitcast.13, s32[2048]{0:T(1024)S(1)} %copy-done.7, f32[128]{0:T(128)S(1)} %get-tuple-element.18), kind=kOutput, calls=%fused_computation.76 | convolution fusion | flops 134676352 | bytes 1517056 | tf_op jit(solution)/shard_map/dot_general | solution.py:305
  179.1 8.4 %mp_gather_sum.3 = (bf16[128,1024]{1,0:T(8,128)(2,1)S(1)}, f32[8,128]{1,0:T(8,128)S(1)}) custom-call(bf16[128,256]{1,0:T(8,128)(2,1)S(1)} %get-tuple-element.25.own_ref, f32[8,128]{1,0:T(8,128)S(1)} %broadcast_in_dim.82.term_ref), custom_call_target="tpu_custom_call" | custom-call | bytes 327680 | tf_op jit(solution)/shard_map/mp_gather_sum/pallas_call | solution.py:190
  187.5 3.3 %convolution_convert_fusion.3.part_ref = bf16[128,1024]{1,0:T(8,128)(2,1)S(1)} fusion(bf16[1024,1024]{1,0:T(8,128)(2,1)S(1)} %copy-done, bf16[1024,1024]{1,0:T(8,128)(2,1)} %param.11, f32[256,1024]{1,0:T(8,128)} %copy-done.4, bf16[128,1024]{1,0:T(8,128)(2,1)S(1)} %get-tuple-element.12, f32[128]{0:T(128)S(1)} %bitcast_multiply_fusion.2, ...), kind=kOutput, calls=%fused_computation.11 | convolution fusion | flops 539099136 | bytes 5506048 | tf_op jit(solution)/shard_map/dot_general | solution.py:234
  190.8 7.7 %mp_scatter.5 = f32[128,256]{1,0:T(8,128)S(1)} custom-call(bf16[128,1024]{1,0:T(8,128)(2,1)S(1)} %convolution_convert_fusion.3.part_ref), custom_call_target="tpu_custom_call" | custom-call | flops 131072 | bytes 524288 | tf_op jit(solution)/shard_map/mp_scatter/pallas_call | solution.py:160
  (59 shorter events, 11.2 us)
Async XLA Ops:
  0.6 3.9 %copy-start = (bf16[1024,1024]{1,0:T(8,128)(2,1)S(1)}, bf16[1024,1024]{1,0:T(8,128)(2,1)}, u32[]{:S(2)}) copy-start(bf16[1024,1024]{1,0:T(8,128)(2,1)} %param.10) | copy-start | bytes 6291460
  2.6 3.7 %copy-start.14 = (bf16[1024,1024]{1,0:T(8,128)(2,1)S(1)}, bf16[1024,1024]{1,0:T(8,128)(2,1)}, u32[]{:S(2)}) copy-start(bf16[1024,1024]{1,0:T(8,128)(2,1)} %param.11) | copy-start | bytes 6291460
  3.7 0.8 copy-start.3
  5.2 1.0 copy-start.4
  7.0 14.5 %copy-start.6 = (s32[2048]{0:T(1024)}, s32[2048]{0:T(1024)S(1)}, u32[]{:S(2)}) copy-start(s32[2048]{0:T(1024)S(1)} %eq.64) | copy-start | bytes 24580
  18.4 22.2 %copy-start.8 = (s32[128,8]{0,1:T(8,128)S(1)}, s32[128,8]{0,1:T(8,128)}, u32[]{:S(2)}) copy-start(s32[128,8]{0,1:T(8,128)} %param.12) | copy-start | bytes 12292
  21.5 74.3 %all-to-all-start = ((bf16[128,16,256]{2,1,0:T(8,128)(2,1)}), bf16[128,16,256]{2,1,0:T(8,128)(2,1)S(1)}, u32[]{:S(2)}, u32[]{:S(2)}) async-start(bf16[128,16,256]{2,1,0:T(8,128)(2,1)} %bitcast.72), calls=%async_computation | async-start | bytes 2097152 | tf_op jit(solution)/shard_map/all_to_all | solution.py:262
  45.6 0.8 copy-start.2
  95.8 5.9 %copy-start.1 = (bf16[128,16,256]{2,1,0:T(8,128)(2,1)}, bf16[128,16,256]{2,1,0:T(8,128)(2,1)S(1)}, u32[]{:S(2)}) copy-start(bf16[128,16,256]{2,1,0:T(8,128)(2,1)S(1)} %all-to-all-done) | copy-start | bytes 3145732
  109.2 1.3 copy-start.9
  109.9 0.6 copy-start.11
  112.8 20.1 %copy-start.10 = (f32[128]{0:T(128)S(1)}, f32[128]{0:T(128)}, u32[]{:S(2)}) copy-start(f32[128]{0:T(128)} %copy-done.9) | copy-start | bytes 1540
  114.3 62.2 %all-to-all-start.1 = ((bf16[128,16,256]{2,1,0:T(8,128)(2,1)}), bf16[128,16,256]{2,1,0:T(8,128)(2,1)}, u32[]{:S(2)}, u32[]{:S(2)}) async-start(bf16[128,16,256]{2,1,0:T(8,128)(2,1)} %bitcast.12), calls=%async_computation.1 | async-start | bytes 2097152 | tf_op jit(solution)/shard_map/all_to_all | solution.py:294
  143.0 33.4 %copy-start.7 = (s32[2048]{0:T(1024)S(1)}, s32[2048]{0:T(1024)}, u32[]{:S(2)}) copy-start(s32[2048]{0:T(1024)} %copy-done.6) | copy-start | bytes 24580
  143.1 33.4 %copy-start.12 = (f32[128]{0:T(128)S(1)}, f32[128]{0:T(128)}, u32[]{:S(2)}) copy-start(f32[128]{0:T(128)} %get-tuple-element.28) | copy-start | bytes 1540
  187.5 11.0 %copy-start.5 = (f32[128,256]{1,0:T(8,128)S(1)}, f32[128,256]{1,0:T(8,128)}, u32[]{:S(2)}) copy-start(f32[128,256]{1,0:T(8,128)} %get-tuple-element.33) | copy-start | bytes 393220
  187.5 11.0 %copy-start.13 = (f32[128]{0:T(128)S(1)}, f32[128]{0:T(128)}, u32[]{:S(2)}) copy-start(f32[128]{0:T(128)} %get-tuple-element.28) | copy-start | bytes 1540

commit v3 on v2

--- a/solution.py
+++ b/solution.py
@@ -236,33 +236,40 @@
     return (summed + grad_out_own).astype(jnp.bfloat16)
 
 
+def encode(states, w_in, w_out, number):
+    pre_act = jnp.dot(states, w_in, preferred_element_type=jnp.float32)
+    hidden = gelu_value(pre_act).astype(jnp.bfloat16)
+    partial_out = jnp.dot(hidden, w_out, preferred_element_type=jnp.float32).astype(jnp.bfloat16)
+    return (pre_act, own_columns(states).astype(jnp.float32) + mp_scatter(partial_out, number))
+
+
 def shards(query_states, passage_states, w_in, w_out, neg_owner, neg_mask, served_rows, loss_scale):
     owners = lax.axis_size("dp")
     row_count = query_states.shape[0]
     capacity = served_rows.shape[2]
     slots = owners * capacity
-    states = jnp.concatenate([passage_states, query_states], axis=0)
-    pre_act = jnp.dot(states, w_in, preferred_element_type=jnp.float32)
-    hidden = gelu_value(pre_act).astype(jnp.bfloat16)
-    partial_out = jnp.dot(hidden, w_out, preferred_element_type=jnp.float32).astype(jnp.bfloat16)
-    out_own = own_columns(states).astype(jnp.float32) + mp_scatter(partial_out, 0)
-    out_pass, out_query = out_own[:row_count], out_own[row_count:]
-    out_half = out_own.astype(jnp.bfloat16)
-    half_pass, half_query = out_half[:row_count], out_half[row_count:]
+    pre_pass, out_pass = encode(passage_states, w_in, w_out, 0)
+    half_pass = out_pass.astype(jnp.bfloat16)
     column_width = half_pass.shape[1]
 
     served = served_rows[0].reshape(-1)
     served_pick = (served[:, None] == jnp.arange(row_count, dtype=jnp.int32)[None, :]).astype(jnp.bfloat16)
-    flat_owner = neg_owner.reshape(-1)
-    onehot = (flat_owner[:, None] == jnp.arange(owners, dtype=jnp.int32)[None, :]).astype(jnp.int32)
-    before = jnp.cumsum(onehot, axis=0, dtype=jnp.int32) - onehot
-    slot_index = jnp.sum(before * onehot, axis=1, dtype=jnp.int32)
-    slot_place = (flat_owner * capacity + slot_index).reshape(neg_owner.shape).T
     outgoing_rows = jnp.dot(served_pick, half_pass, preferred_element_type=jnp.float32).astype(jnp.bfloat16)
+    query_states, outgoing_rows = lax.optimization_barrier((query_states, outgoing_rows))
     slot_rows = lax.all_to_all(
         outgoing_rows.reshape(owners, capacity, column_width), "dp", split_axis=0, concat_axis=0, tiled=True
     ).reshape(slots, column_width)
-    out_full = mp_gather(out_half, 1)
+    pre_query, out_query = encode(query_states, w_in, w_out, 7)
+    half_query = out_query.astype(jnp.bfloat16)
+    out_full = mp_gather(jnp.concatenate([half_pass, half_query], axis=0), 1)
+    owner_rows = neg_owner.T
+    named = owner_rows[:, :, None] == jnp.arange(owners, dtype=jnp.int32)[None, None, :]
+    names = jnp.any(named, axis=0).astype(jnp.bfloat16)
+    spot = jnp.arange(row_count, dtype=jnp.int32)
+    earlier = (spot[None, :] < spot[:, None]).astype(jnp.bfloat16)
+    before = jnp.dot(earlier, names, preferred_element_type=jnp.float32)
+    slot_index = jnp.sum(jnp.where(named, before[None, :, :], 0.0), axis=2).astype(jnp.int32)
+    slot_place = owner_rows * capacity + slot_index
     slot_hit = slot_place[:, :, None] == jnp.arange(slots, dtype=jnp.int32)[None, None, :]
 
     slot_part = lax.dot_general(half_query, slot_rows, (((1,), (1,)), ((), ())), preferred_element_type=jnp.float32)
@@ -271,7 +278,7 @@
     neg_part = jnp.sum(jnp.where(slot_hit, slot_part[None, :, :], 0.0), axis=2)
     neg_square = jnp.sum(jnp.where(slot_hit, slot_square[None, None, :], 0.0), axis=2)
     pos_part = jnp.sum(half_query.astype(jnp.float32) * half_pass.astype(jnp.float32), axis=1)
-    squares = jnp.sum(out_own * out_own, axis=1).reshape(2, row_count)
+    squares = jnp.stack([jnp.sum(out_pass * out_pass, axis=1), jnp.sum(out_query * out_query, axis=1)])
     extra = jnp.concatenate([pos_part[None, :], squares, jnp.zeros((5, row_count), jnp.float32)], axis=0)
     sums = mp_sum(jnp.concatenate([neg_part, neg_square, extra], axis=0), 2)
     negatives = neg_owner.shape[1]
@@ -299,7 +306,7 @@
         slot_weight.astype(jnp.bfloat16), slot_rows, preferred_element_type=jnp.float32
     )
     grad_query_states = decode(
-        grad_query_emb, pre_act[row_count:], out_query, out_full[row_count:], inv_query, w_in, w_out, 3
+        grad_query_emb, pre_query, out_query, out_full[row_count:], inv_query, w_in, w_out, 3
     )
     returned, grad_query_states = lax.optimization_barrier((returned, grad_query_states))
     gathered_back = lax.dot_general(
@@ -307,7 +314,7 @@
     )
     grad_pass_emb = (grad_pos * inv_query)[:, None] * out_query + gathered_back
     grad_passage_states = decode(
-        grad_pass_emb, pre_act[:row_count], out_pass, out_full[:row_count], inv_pass, w_in, w_out, 5
+        grad_pass_emb, pre_pass, out_pass, out_full[:row_count], inv_pass, w_in, w_out, 5
     )
     return (grad_query_states, grad_passage_states)
 

time: 200 us -> 192 us (0.960)
  local copies, waits for them, and re-layouts: 13.1 us -> 3.84 us
  Pallas kernels: 59.3 us -> 64.3 us
  waiting for transfers between devices: 66.1 us -> 63 us
  other arithmetic: 16.6 us -> 14.3 us
    pallas_call x3 -> x4, Pallas kernels: 26.3 us -> 31.3 us  [mp_scatter(): pl.pallas_call(functools.partial(scatter_kernel, ways), out_shape=jax.Sha...]
    all_to_all x1, waiting for transfers between devices: 44.9 us -> 41.4 us  [shards(): lax.all_to_all(outgoing_rows.reshape(owners, capacity, column_width), 'dp...]
    dot_general x2 -> x5, matrix products: 1.41 us -> 4.14 us  [the longest x2 3.08 us: encode(): pre_act = jnp.dot(states, w_in, preferred_element_type=jnp.float32)]
    eq x3 -> x0, local copies, waits for them, and re-layouts: 2.59 us -> none  [shards(): flat_owner[:, None] == jnp.arange(owners, dtype=jnp.int32)[None, :]]
    unnamed x33, local copies, waits for them, and re-layouts: 5.29 us -> 2.97 us
    another operation x3 -> x0, other arithmetic: 2.14 us -> none
  transfers between devices with their start and end apart: 2 -> 2, of which waited for: 2 -> 2; matrix products, arithmetic and copies ran while one was open for 8% -> 6% of each run, Pallas kernels for 13% -> 18%
where the time goes in v3:
time: 192 us; the launch traced here: 191 us
  Pallas kernels  64.3 us (33%)
  waiting for transfers between devices  63 us (33%)
  starting transfers between devices  26.3 us (14%)
  matrix products  17.7 us (9%)
  other arithmetic  14.3 us (7%)
  local copies, waits for them, and re-layouts  3.84 us (2%)
    all_to_all x1, waiting for transfers between devices, shards(): lax.all_to_all(outgoing_rows.reshape(owners, capacity, column_width), 'dp...  41.4 us
    pallas_call x4, Pallas kernels, mp_scatter(): pl.pallas_call(functools.partial(scatter_kernel, ways), out_shape=jax.Sha...  31.3 us
    all_to_all x1, waiting for transfers between devices, shards(): lax.all_to_all(outgoing_grad.reshape(owners, capacity, column_width), 'dp...  21.6 us
    all_to_all x1, starting transfers between devices, shards(): lax.all_to_all(outgoing_rows.reshape(owners, capacity, column_width), 'dp...  19 us
    pallas_call x2, Pallas kernels, mp_gather_sum(): pl.pallas_call(functools.partial(gather_sum_kernel, ways), out_shape=(jax...  16.3 us
    pallas_call x1, Pallas kernels, mp_gather(): pl.pallas_call(functools.partial(gather_kernel, ways), out_shape=jax.Shap...  10.6 us
    all_to_all x1, starting transfers between devices, shards(): lax.all_to_all(outgoing_grad.reshape(owners, capacity, column_width), 'dp...  7.29 us
    dot_general x2, matrix products, decode(): lax.dot_general(grad_pre, w_in, contract, preferred_element_type=jnp.floa...  6.49 us
  transfers between devices with their start and end apart: 2, of which 2 were waited for; matrix products, arithmetic and copies ran while one was open for 6% of the time, Pallas kernels for 18%

profile of v3, /device:TPU:32, one launch (start us, length us, event | category | flops | bytes accessed | tf_op | source)
XLA Modules:
  0.0 191.1 jit_solution(5838361766825053563)
XLA Ops:
  0.6 1.6 copy-done
  2.2 1.5 fusion.55
  3.8 0.8 copy-done.4
  5.0 8.5 %mp_scatter.4 = f32[128,256]{1,0:T(8,128)S(1)} custom-call(bf16[128,1024]{1,0:T(8,128)(2,1)S(1)} %convolution_convert_fusion.5.part_ref), custom_call_target="tpu_custom_call" | custom-call | flops 131072 | bytes 524288 | tf_op jit(solution)/shard_map/mp_scatter/pallas_call | solution.py:160
  13.5 1.6 multiply_reduce_fusion.4
  15.3 1.5 convolution_convert_fusion.1
  16.8 19.0 %all-to-all-start = ((bf16[128,16,256]{2,1,0:T(8,128)(2,1)}), bf16[128,16,256]{2,1,0:T(8,128)(2,1)S(1)}, u32[]{:S(2)}, u32[]{:S(2)}) async-start(bf16[128,16,256]{2,1,0:T(8,128)(2,1)} %bitcast.70), calls=%async_computation | async-start | bytes 2097152 | tf_op jit(solution)/shard_map/all_to_all | solution.py:259
  35.8 1.5 fusion.56
  38.3 7.8 %mp_scatter.5 = f32[128,256]{1,0:T(8,128)S(1)} custom-call(bf16[128,1024]{1,0:T(8,128)(2,1)S(1)} %convolution_convert_fusion.4.part_ref), custom_call_target="tpu_custom_call" | custom-call | flops 131072 | bytes 524288 | tf_op jit(solution)/shard_map/mp_scatter/pallas_call | solution.py:160
  47.5 1.5 multiply_reduce_fusion.3
  49.0 0.6 multiply_reduce_fusion.5
  49.6 41.4 %all-to-all-done = bf16[128,16,256]{2,1,0:T(8,128)(2,1)S(1)} async-done(((bf16[128,16,256]{2,1,0:T(8,128)(2,1)}), bf16[128,16,256]{2,1,0:T(8,128)(2,1)S(1)}, u32[]{:S(2)}, u32[]{:S(2)}) %all-to-all-start) | async-done | bytes 1048608 | tf_op jit(solution)/shard_map/all_to_all | solution.py:259
  92.0 2.8 %select_reduce_fusion.2 = (f32[8,128]{1,0:T(8,128)S(1)}, f32[8,128]{1,0:T(8,128)S(1)}) fusion(f32[2048]{0:T(1024)S(1)} %broadcast_in_dim.93, s32[8,128]{1,0:T(8,128)S(1)} %convert_add_fusion.2, f32[128,2048]{1,0:T(8,128)S(1)} %fusion.57), kind=kLoop, calls=%fused_computation.2 | loop fusion | flops 10483712 | bytes 1069056 | tf_op jit(solution)/shard_map/reduce_sum | solution.py:279
  94.9 0.7 concatenate.6.term_ref
  95.5 6.1 %mp_sum.1 = f32[24,128]{1,0:T(8,128)S(1)} custom-call(f32[24,128]{1,0:T(8,128)S(1)} %concatenate.6.term_ref), custom_call_target="tpu_custom_call" | custom-call | bytes 61440 | tf_op jit(solution)/shard_map/mp_sum/pallas_call | solution.py:207
  101.7 0.7 fusion.54
  102.4 0.6 fusion.53
  103.0 2.4 %select_reduce_fusion = (bf16[128,2048]{1,0:T(8,128)(2,1)S(1)}, bf16[128,2048]{1,0:T(8,128)(2,1)S(1)}) fusion(f32[8,128]{1,0:T(8,128)S(1)} %get-tuple-element.39, s32[8,128]{1,0:T(8,128)S(1)} %convert_add_fusion.2, f32[8,128]{1,0:T(8,128)S(1)} %get-tuple-element.38), kind=kLoop, calls=%fused_computation | loop fusion | flops 9961472 | bytes 1060864 | tf_op jit(solution)/shard_map/reduce_sum | solution.py:304
  105.4 1.4 convolution_convert_fusion
  106.8 7.3 %all-to-all-start.1 = ((bf16[128,16,256]{2,1,0:T(8,128)(2,1)}), bf16[128,16,256]{2,1,0:T(8,128)(2,1)}, u32[]{:S(2)}, u32[]{:S(2)}) async-start(bf16[128,16,256]{2,1,0:T(8,128)(2,1)} %bitcast.10), calls=%async_computation.1 | async-start | bytes 2097152 | tf_op jit(solution)/shard_map/all_to_all | solution.py:301
  114.1 10.6 %mp_gather.1 = bf16[256,1024]{1,0:T(8,128)(2,1)S(1)} custom-call(bf16[256,256]{1,0:T(8,128)(2,1)S(1)} %pad_maximum_fusion.own_ref), custom_call_target="tpu_custom_call" | custom-call | bytes 655360 | tf_op jit(solution)/shard_map/mp_gather/pallas_call | solution.py:175
  125.3 1.6 multiply_reduce_fusion.2
  127.0 7.9 %mp_gather_sum.2 = (bf16[128,1024]{1,0:T(8,128)(2,1)S(1)}, f32[8,128]{1,0:T(8,128)S(1)}) custom-call(bf16[128,256]{1,0:T(8,128)(2,1)S(1)} %get-tuple-element.35.own_ref, f32[8,128]{1,0:T(8,128)S(1)} %broadcast_in_dim.99.term_ref), custom_call_target="tpu_custom_call" | custom-call | bytes 327680 | tf_op jit(solution)/shard_map/mp_gather_sum/pallas_call | solution.py:190
  135.4 3.3 %convolution_convert_fusion.3.part_ref = bf16[128,1024]{1,0:T(8,128)(2,1)S(1)} fusion(bf16[1024,1024]{1,0:T(8,128)(2,1)S(1)} %copy-done, bf16[1024,1024]{1,0:T(8,128)(2,1)} %param.11, f32[128,1024]{1,0:T(8,128)} %copy-done.5, bf16[128,1024]{1,0:T(8,128)(2,1)S(1)} %get-tuple-element.12, f32[128]{0:T(128)} %bitcast_multiply_fusion.5, ...), kind=kOutput, calls=%fused_computation.11 | convolution fusion | flops 539099136 | bytes 5506048 | tf_op jit(solution)/shard_map/dot_general | solution.py:234
  138.7 7.3 %mp_scatter.6 = f32[128,256]{1,0:T(8,128)S(1)} custom-call(bf16[128,1024]{1,0:T(8,128)(2,1)S(1)} %convolution_convert_fusion.3.part_ref), custom_call_target="tpu_custom_call" | custom-call | flops 131072 | bytes 524288 | tf_op jit(solution)/shard_map/mp_scatter/pallas_call | solution.py:160
  146.0 1.4 add_convert_fusion.1
  147.4 21.6 %all-to-all-done.1 = bf16[128,16,256]{2,1,0:T(8,128)(2,1)} async-done(((bf16[128,16,256]{2,1,0:T(8,128)(2,1)}), bf16[128,16,256]{2,1,0:T(8,128)(2,1)}, u32[]{:S(2)}, u32[]{:S(2)}) %all-to-all-start.1) | async-done | bytes 1048608 | tf_op jit(solution)/shard_map/all_to_all | solution.py:301
  169.0 2.1 %multiply_reduce_fusion.1 = (f32[128]{0:T(128)S(1)}, bf16[128,256]{1,0:T(8,128)(2,1)S(1)}, f32[128,256]{1,0:T(8,128)S(1)}) fusion(f32[128,256]{1,0:T(8,128)S(1)} %get-tuple-element.29, f32[128]{0:T(128)} %get-tuple-element.36, bf16[2048,256]{1,0:T(8,128)(2,1)} %bitcast.11, s32[2048]{0:T(1024)} %copy-done.8, f32[128,256]{1,0:T(8,128)S(1)} %get-tuple-element.27, ...), kind=kOutput, calls=%fused_computation.60 | convolution fusion | flops 134676352 | bytes 1517056 | tf_op jit(solution)/shard_map/dot_general | solution.py:312
  171.1 8.4 %mp_gather_sum.3 = (bf16[128,1024]{1,0:T(8,128)(2,1)S(1)}, f32[8,128]{1,0:T(8,128)S(1)}) custom-call(bf16[128,256]{1,0:T(8,128)(2,1)S(1)} %get-tuple-element.33.own_ref, f32[8,128]{1,0:T(8,128)S(1)} %broadcast_in_dim.100.term_ref), custom_call_target="tpu_custom_call" | custom-call | bytes 327680 | tf_op jit(solution)/shard_map/mp_gather_sum/pallas_call | solution.py:190
  179.5 3.2 %convolution_convert_fusion.2.part_ref = bf16[128,1024]{1,0:T(8,128)(2,1)S(1)} fusion(bf16[1024,1024]{1,0:T(8,128)(2,1)S(1)} %copy-done, bf16[1024,1024]{1,0:T(8,128)(2,1)} %param.11, f32[128,1024]{1,0:T(8,128)} %copy-done.4, bf16[128,1024]{1,0:T(8,128)(2,1)S(1)} %get-tuple-element.16, f32[128]{0:T(128)S(1)} %bitcast_multiply_fusion.2, ...), kind=kOutput, calls=%fused_computation.10 | convolution fusion | flops 539099136 | bytes 5506048 | tf_op jit(solution)/shard_map/dot_general | solution.py:234
  182.7 7.7 %mp_scatter.7 = f32[128,256]{1,0:T(8,128)S(1)} custom-call(bf16[128,1024]{1,0:T(8,128)(2,1)S(1)} %convolution_convert_fusion.2.part_ref), custom_call_target="tpu_custom_call" | custom-call | flops 131072 | bytes 524288 | tf_op jit(solution)/shard_map/mp_scatter/pallas_call | solution.py:160
  190.4 0.7 add_convert_fusion
  (54 shorter events, 4.4 us)
Async XLA Ops:
  0.6 1.6 copy-start
  2.2 2.3 %copy-start.2 = (bf16[1024,1024]{1,0:T(8,128)(2,1)S(1)}, bf16[1024,1024]{1,0:T(8,128)(2,1)}, u32[]{:S(2)}) copy-start(bf16[1024,1024]{1,0:T(8,128)(2,1)} %param.11) | copy-start | bytes 6291460
  3.8 0.8 copy-start.4
  4.6 10.5 %copy-start.10 = (s32[1,128,16]{1,2,0:T(8,128)S(1)}, s32[1,128,16]{1,2,0:T(8,128)}, u32[]{:S(2)}) copy-start(s32[1,128,16]{1,2,0:T(8,128)} %param.14) | copy-start | bytes 24580
  15.1 22.3 %copy-start.6 = (bf16[128,256]{1,0:T(8,128)(2,1)}, bf16[128,256]{1,0:T(8,128)(2,1)S(1)}, u32[]{:S(2)}) copy-start(bf16[128,256]{1,0:T(8,128)(2,1)S(1)} %convert_element_type.106) | copy-start | bytes 196612
  15.3 1.5 copy-start.8
  16.8 74.3 %all-to-all-start = ((bf16[128,16,256]{2,1,0:T(8,128)(2,1)}), bf16[128,16,256]{2,1,0:T(8,128)(2,1)S(1)}, u32[]{:S(2)}, u32[]{:S(2)}) async-start(bf16[128,16,256]{2,1,0:T(8,128)(2,1)} %bitcast.70), calls=%async_computation | async-start | bytes 2097152 | tf_op jit(solution)/shard_map/all_to_all | solution.py:259
  35.8 1.7 copy-start.3
  37.5 0.8 copy-start.5
  37.5 9.3 %copy-start.9 = (s32[128,8]{0,1:T(8,128)S(1)}, s32[128,8]{0,1:T(8,128)}, u32[]{:S(2)}) copy-start(s32[128,8]{0,1:T(8,128)} %param.12) | copy-start | bytes 12292
  91.1 3.8 %copy-start.1 = (bf16[128,16,256]{2,1,0:T(8,128)(2,1)}, bf16[128,16,256]{2,1,0:T(8,128)(2,1)S(1)}, u32[]{:S(2)}) copy-start(bf16[128,16,256]{2,1,0:T(8,128)(2,1)S(1)} %all-to-all-done) | copy-start | bytes 3145732
  91.5 3.3 %copy-start.15 = (f32[128]{0:T(128)S(1)}, f32[128]{0:T(128)}, u32[]{:S(2)}) copy-start(f32[128]{0:T(128)} %get-tuple-element.30) | copy-start | bytes 1540
  101.7 1.3 copy-start.11
  102.4 0.6 copy-start.13
  105.3 8.8 %copy-start.7 = (bf16[128,256]{1,0:T(8,128)(2,1)S(1)}, bf16[128,256]{1,0:T(8,128)(2,1)}, u32[]{:S(2)}) copy-start(bf16[128,256]{1,0:T(8,128)(2,1)} %copy-done.6) | copy-start | bytes 196612
  105.4 19.4 %copy-start.14 = (f32[128]{0:T(128)S(1)}, f32[128]{0:T(128)}, u32[]{:S(2)}) copy-start(f32[128]{0:T(128)} %copy-done.13) | copy-start | bytes 1540
  106.8 62.2 %all-to-all-start.1 = ((bf16[128,16,256]{2,1,0:T(8,128)(2,1)}), bf16[128,16,256]{2,1,0:T(8,128)(2,1)}, u32[]{:S(2)}, u32[]{:S(2)}) async-start(bf16[128,16,256]{2,1,0:T(8,128)(2,1)} %bitcast.10), calls=%async_computation.1 | async-start | bytes 2097152 | tf_op jit(solution)/shard_map/all_to_all | solution.py:301
  179.4 10.9 %copy-start.12 = (f32[128]{0:T(128)S(1)}, f32[128]{0:T(128)}, u32[]{:S(2)}) copy-start(f32[128]{0:T(128)} %get-tuple-element.36) | copy-start | bytes 1540

commit v4 on v3

--- a/solution.py
+++ b/solution.py
@@ -142,6 +142,108 @@
     sum_ref[...] = total
 
 
+def column_kernel(ways, plane, parts, block_ref, part_ref, column_ref, out_ref, landed, mp_send, mp_recv, up_send, up_recv, down_send, down_recv):
+    depth, rows = column_ref.shape[0], column_ref.shape[1]
+    width = out_ref.shape[1]
+    piece = rows // parts
+    me, place = lax.axis_index("mp"), lax.axis_index("dp")
+    count = depth * plane
+    high, here = place // plane, lax.rem(place, plane)
+    above = lax.rem(place + plane, count)
+    below = lax.rem(place + count - plane, count)
+    barrier = pltpu.get_barrier_semaphore()
+    for step in range(1, ways):
+        pl.semaphore_signal(
+            barrier, inc=1, device_id={"mp": lax.rem(me + step, ways)}, device_id_type=pl.DeviceIdType.MESH
+        )
+    for neighbour in (above, below):
+        pl.semaphore_signal(barrier, inc=1, device_id={"dp": neighbour}, device_id_type=pl.DeviceIdType.MESH)
+    pl.semaphore_wait(barrier, ways + 1)
+
+    def hop(step, part, upward):
+        rank = lax.rem(high + depth - (step - 1), depth) if upward else lax.rem(high + step - 1, depth)
+        span = pl.ds(part * piece, piece)
+        target = column_ref.at[rank, span]
+        return pltpu.make_async_remote_copy(
+            src_ref=block_ref.at[span] if step == 1 else target,
+            dst_ref=target,
+            send_sem=(up_send if upward else down_send).at[(step - 1) * parts + part],
+            recv_sem=(up_recv if upward else down_recv).at[(step - 1) * parts + part],
+            device_id={"dp": above if upward else below},
+            device_id_type=pl.DeviceIdType.MESH,
+        )
+
+    up_steps, down_steps = depth // 2, depth - 1 - depth // 2
+    hops = {}
+    for part in range(parts):
+        for upward in (True, False):
+            hops[1, part, upward] = hop(1, part, upward)
+            hops[1, part, upward].start()
+    copies = []
+    for step in range(1, ways):
+        peer = lax.rem(me + step, ways)
+        copy = remote(
+            block_of(part_ref, peer, width),
+            landed.at[step - 1],
+            mp_send.at[step - 1],
+            mp_recv.at[step - 1],
+            peer,
+        )
+        copy.start()
+        copies.append(copy)
+    column_ref[high] = block_ref[...]
+    for step in range(2, up_steps + 1):
+        for part in range(parts):
+            for upward in (True, False):
+                hops[step - 1, part, upward].wait_recv() if (step - 1, part, upward) in hops else None
+                if upward or step <= down_steps:
+                    hops[step, part, upward] = hop(step, part, upward)
+                    hops[step, part, upward].start()
+    for copy in copies:
+        copy.wait()
+    own = part_ref[:, pl.ds(pl.multiple_of(me * width, 128), width)]
+    total = own.astype(jnp.float32)
+    for step in range(1, ways):
+        total = total + landed[step - 1].astype(jnp.float32)
+    out_ref[...] = total
+    for (step, part, upward), copy in hops.items():
+        if step == up_steps:
+            copy.wait_recv()
+        copy.wait_send()
+
+
+def plane_kernel(plane, capacity, rows_ref, out_ref, send_sem, recv_sem):
+    place = lax.axis_index("dp")
+    here = lax.rem(place, plane)
+    base = place - here
+    barrier = pltpu.get_barrier_semaphore()
+    for step in range(1, plane):
+        pl.semaphore_signal(
+            barrier,
+            inc=1,
+            device_id={"dp": base + lax.rem(here + step, plane)},
+            device_id_type=pl.DeviceIdType.MESH,
+        )
+    pl.semaphore_wait(barrier, plane - 1)
+    own = pl.ds(pl.multiple_of(here * capacity, capacity), capacity)
+    copies = []
+    for step in range(1, plane):
+        peer = lax.rem(here + step, plane)
+        copy = pltpu.make_async_remote_copy(
+            src_ref=rows_ref.at[:, pl.ds(pl.multiple_of(peer * capacity, capacity), capacity)],
+            dst_ref=out_ref.at[:, own],
+            send_sem=send_sem.at[step - 1],
+            recv_sem=recv_sem.at[step - 1],
+            device_id={"dp": base + peer},
+            device_id_type=pl.DeviceIdType.MESH,
+        )
+        copy.start()
+        copies.append(copy)
+    out_ref[:, own] = rows_ref[:, own]
+    for copy in copies:
+        copy.wait()
+
+
 def in_vmem(count):
     return [pl.BlockSpec(memory_space=pltpu.VMEM)] * count
 
@@ -216,6 +318,47 @@
     )(term)
 
 
+def column_gather(block, part, plane, parts, number):
+    ways = lax.axis_size("mp")
+    depth = lax.axis_size("dp") // plane
+    rows, width = part.shape[0], part.shape[1] // ways
+    up_steps, down_steps = depth // 2, depth - 1 - depth // 2
+    sem = pltpu.SemaphoreType.DMA
+    return pl.pallas_call(
+        functools.partial(column_kernel, ways, plane, parts),
+        out_shape=(
+            jax.ShapeDtypeStruct((depth,) + block.shape, block.dtype),
+            jax.ShapeDtypeStruct((rows, width), jnp.float32),
+        ),
+        in_specs=in_vmem(2),
+        out_specs=tuple(in_vmem(2)),
+        scratch_shapes=[pltpu.VMEM((ways - 1, rows, width), part.dtype)]
+        + sems(ways)
+        + [sem((up_steps * parts,)), sem((up_steps * parts,)), sem((down_steps * parts,)), sem((down_steps * parts,))],
+        compiler_params=params(number),
+        name="column_gather",
+    )(block, part)
+
+
+def plane_exchange(rows, plane, capacity, number):
+    sem = pltpu.SemaphoreType.DMA
+    return pl.pallas_call(
+        functools.partial(plane_kernel, plane, capacity),
+        out_shape=jax.ShapeDtypeStruct(rows.shape, rows.dtype),
+        in_specs=in_vmem(1),
+        out_specs=pl.BlockSpec(memory_space=pltpu.VMEM),
+        scratch_shapes=[sem((plane - 1,)), sem((plane - 1,))],
+        compiler_params=params(number),
+        name="plane_exchange",
+    )(rows)
+
+
+def encode_part(states, w_in, w_out):
+    pre_act = jnp.dot(states, w_in, preferred_element_type=jnp.float32)
+    hidden = gelu_value(pre_act).astype(jnp.bfloat16)
+    return (pre_act, jnp.dot(hidden, w_out, preferred_element_type=jnp.float32).astype(jnp.bfloat16))
+
+
 def decode(grad_own, pre_act, out_own, out_full, inv_norm, w_in, w_out, number):
     inv = inv_norm[:, None]
     unit_own = out_own * inv
@@ -254,12 +397,32 @@
 
     served = served_rows[0].reshape(-1)
     served_pick = (served[:, None] == jnp.arange(row_count, dtype=jnp.int32)[None, :]).astype(jnp.bfloat16)
-    outgoing_rows = jnp.dot(served_pick, half_pass, preferred_element_type=jnp.float32).astype(jnp.bfloat16)
-    query_states, outgoing_rows = lax.optimization_barrier((query_states, outgoing_rows))
-    slot_rows = lax.all_to_all(
-        outgoing_rows.reshape(owners, capacity, column_width), "dp", split_axis=0, concat_axis=0, tiled=True
-    ).reshape(slots, column_width)
-    pre_query, out_query = encode(query_states, w_in, w_out, 7)
+    plane, depth = 8, owners // 8
+    block = jnp.concatenate(
+        [
+            half_pass,
+            served.astype(jnp.bfloat16).reshape(-1, column_width),
+            jnp.zeros((16 - served.shape[0] // column_width, column_width), jnp.bfloat16),
+        ],
+        axis=0,
+    )
+    pre_query, part_query = encode_part(query_states, w_in, w_out)
+    column, sum_query = column_gather(block, part_query, plane, 3, 7)
+    out_query = own_columns(query_states).astype(jnp.float32) + sum_query
+    start = (lax.axis_index("dp") // plane) * plane * capacity
+    served_here = lax.dynamic_slice(
+        column,
+        (0, row_count + start // column_width, lax.rem(start, column_width)),
+        (depth, 1, plane * capacity),
+    ).reshape(depth, plane * capacity)
+    wanted = served_here.astype(jnp.int32)[:, :, None] == jnp.arange(row_count, dtype=jnp.int32)[None, None, :]
+    chosen = lax.dot_general(
+        wanted.astype(jnp.bfloat16),
+        column[:, :row_count],
+        (((2,), (1,)), ((0,), (0,))),
+        preferred_element_type=jnp.float32,
+    ).astype(jnp.bfloat16)
+    slot_rows = plane_exchange(chosen, plane, capacity, 8).reshape(slots, column_width)
     half_query = out_query.astype(jnp.bfloat16)
     out_full = mp_gather(jnp.concatenate([half_pass, half_query], axis=0), 1)
     owner_rows = neg_owner.T

time: 192 us -> 178 us (0.927)
  Pallas kernels: 64.3 us -> 109 us
  waiting for transfers between devices: 63 us -> 20.6 us
  starting transfers between devices: 26.3 us -> 11.1 us
    pallas_call x0 -> x2, Pallas kernels: none -> 53.4 us  [the longest x1 37.6 us: column_gather(): pl.pallas_call(functools.partial(column_kernel, ways, plane, parts), out_...]
    all_to_all x1 -> x0, waiting for transfers between devices: 41.4 us -> none  [shards(): lax.all_to_all(outgoing_rows.reshape(owners, capacity, column_width), 'dp...]
    all_to_all x1 -> x0, starting transfers between devices: 19 us -> none  [shards(): lax.all_to_all(outgoing_rows.reshape(owners, capacity, column_width), 'dp...]
    pallas_call x4 -> x3, Pallas kernels: 31.3 us -> 23.2 us  [mp_scatter(): pl.pallas_call(functools.partial(scatter_kernel, ways), out_shape=jax.Sha...]
    all_to_all x1, starting transfers between devices: 7.29 us -> 11.1 us  [shards(): lax.all_to_all(outgoing_grad.reshape(owners, capacity, column_width), 'dp...]
  transfers between devices with their start and end apart: 2 -> 1, of which waited for: 2 -> 1; matrix products, arithmetic and copies ran while one was open for 6% -> 5% of each run, Pallas kernels for 18% -> 14%
where the time goes in v4:
time: 178 us; the launch traced here: 177 us
  Pallas kernels  109 us (61%)
  waiting for transfers between devices  20.6 us (12%)
  matrix products  16.4 us (9%)
  other arithmetic  13.5 us (8%)
  starting transfers between devices  11.1 us (6%)
  local copies, waits for them, and re-layouts  4.25 us (2%)
  between operations  1.8 us (1%)
    pallas_call x1, Pallas kernels, column_gather(): pl.pallas_call(functools.partial(column_kernel, ways, plane, parts), out_...  37.6 us
    pallas_call x3, Pallas kernels, mp_scatter(): pl.pallas_call(functools.partial(scatter_kernel, ways), out_shape=jax.Sha...  23.2 us
    all_to_all x1, waiting for transfers between devices, shards(): lax.all_to_all(outgoing_grad.reshape(owners, capacity, column_width), 'dp...  20.6 us
    pallas_call x2, Pallas kernels, mp_gather_sum(): pl.pallas_call(functools.partial(gather_sum_kernel, ways), out_shape=(jax...  15.8 us
    pallas_call x1, Pallas kernels, plane_exchange(): pl.pallas_call(functools.partial(plane_kernel, plane, capacity), out_shap...  15.8 us
    all_to_all x1, starting transfers between devices, shards(): lax.all_to_all(outgoing_grad.reshape(owners, capacity, column_width), 'dp...  11.1 us
    pallas_call x1, Pallas kernels, mp_gather(): pl.pallas_call(functools.partial(gather_kernel, ways), out_shape=jax.Shap...  10.6 us
    dot_general x2, matrix products, decode(): lax.dot_general(grad_pre, w_in, contract, preferred_element_type=jnp.floa...  6.62 us
  transfers between devices with their start and end apart: 1, of which 1 were waited for; matrix products, arithmetic and copies ran while one was open for 5% of the time, Pallas kernels for 14%

profile of v4, /device:TPU:32, one launch (start us, length us, event | category | flops | bytes accessed | tf_op | source)
XLA Modules:
  0.0 176.8 jit_solution(8536424581113006588)
XLA Ops:
  0.7 1.5 copy-done
  2.2 1.5 fusion.56
  3.8 0.8 copy-done.7
  5.1 8.5 %mp_scatter.3 = f32[128,256]{1,0:T(8,128)S(1)} custom-call(bf16[128,1024]{1,0:T(8,128)(2,1)S(1)} %convolution_convert_fusion.5.part_ref), custom_call_target="tpu_custom_call" | custom-call | flops 131072 | bytes 524288 | tf_op jit(solution)/shard_map/mp_scatter/pallas_call | solution.py:262
  13.6 1.0 multiply_reduce_fusion.4
  15.3 0.8 copy-done.8
  16.1 0.5 copy-done.4
  17.3 37.6 %column_gather.1 = (bf16[16,144,256]{2,1,0:T(8,128)(2,1)S(1)}, f32[128,256]{1,0:T(8,128)S(1)}) custom-call(bf16[144,256]{1,0:T(8,128)(2,1)S(1)} %maximum_maximum_fusion.block_ref, bf16[128,1024]{1,0:T(8,128)(2,1)S(1)} %convolution_convert_fusion.4.part_ref), custom_call_target="tpu_custom_call" | custom-call | tf_op jit(solution)/shard_map/column_gather/pallas_call | solution.py:327
  54.9 0.7 convolution_convert_fusion.1.rows_ref
  55.7 15.8 %plane_exchange.1 = bf16[16,128,256]{2,1,0:T(8,128)(2,1)S(1)} custom-call(bf16[16,128,256]{2,1,0:T(8,128)(2,1)S(1)} %convolution_convert_fusion.1.rows_ref), custom_call_target="tpu_custom_call" | custom-call | tf_op jit(solution)/shard_map/plane_exchange/pallas_call | solution.py:345
  71.5 1.0 multiply_reduce_fusion.3
  73.7 0.5 fusion.58
  74.2 2.8 %select_reduce_fusion.2 = (f32[8,128]{1,0:T(8,128)S(1)}, f32[8,128]{1,0:T(8,128)S(1)}) fusion(f32[2048]{0:T(1024)S(1)} %bitcast.73, s32[8,128]{1,0:T(8,128)S(1)} %convert_add_fusion.2, f32[128,2048]{1,0:T(8,128)S(1)} %fusion.58), kind=kLoop, calls=%fused_computation.2 | loop fusion | flops 10483712 | bytes 1069056 | tf_op jit(solution)/shard_map/reduce_sum | solution.py:442
  77.0 6.1 %mp_sum.1 = f32[24,128]{1,0:T(8,128)S(1)} custom-call(f32[24,128]{1,0:T(8,128)S(1)} %concatenate.10.term_ref), custom_call_target="tpu_custom_call" | custom-call | bytes 61440 | tf_op jit(solution)/shard_map/mp_sum/pallas_call | solution.py:309
  83.9 0.5 fusion.54
  84.4 3.1 %select_reduce_fusion = (bf16[128,2048]{1,0:T(8,128)(2,1)}, bf16[128,2048]{1,0:T(8,128)(2,1)S(1)}) fusion(f32[8,128]{1,0:T(8,128)S(1)} %get-tuple-element.39, s32[8,128]{1,0:T(8,128)S(1)} %convert_add_fusion.2, f32[8,128]{1,0:T(8,128)S(1)} %get-tuple-element.38), kind=kLoop, calls=%fused_computation | loop fusion | flops 9961472 | bytes 1060864 | tf_op jit(solution)/shard_map/reduce_sum | solution.py:467
  87.5 1.5 convolution_convert_fusion
  89.0 11.1 %all-to-all-start = ((bf16[128,16,256]{2,1,0:T(8,128)(2,1)}), bf16[128,16,256]{2,1,0:T(8,128)(2,1)}, u32[]{:S(2)}, u32[]{:S(2)}) async-start(bf16[128,16,256]{2,1,0:T(8,128)(2,1)} %bitcast.70), calls=%async_computation | async-start | bytes 2097152 | tf_op jit(solution)/shard_map/all_to_all | solution.py:464
  100.1 0.9 pad_maximum_fusion.own_ref
  101.0 10.6 %mp_gather.1 = bf16[256,1024]{1,0:T(8,128)(2,1)S(1)} custom-call(bf16[256,256]{1,0:T(8,128)(2,1)S(1)} %pad_maximum_fusion.own_ref), custom_call_target="tpu_custom_call" | custom-call | bytes 655360 | tf_op jit(solution)/shard_map/mp_gather/pallas_call | solution.py:277
  111.6 0.6 bitcast_multiply_fusion.4
  112.2 2.0 %multiply_reduce_fusion.2 = (f32[128]{0:T(128)S(1)}, bf16[128,256]{1,0:T(8,128)(2,1)S(1)}, f32[128,256]{1,0:T(8,128)}) fusion(f32[128,256]{1,0:T(8,128)S(1)} %get-tuple-element.27, f32[128]{0:T(128)S(1)} %fusion.53, bf16[128,2048]{1,0:T(8,128)(2,1)} %get-tuple-element.18, bf16[2048,256]{1,0:T(8,128)(2,1)S(1)} %bitcast.69, ...), kind=kOutput, calls=%fused_computation.64 | convolution fusion | flops 134414208 | bytes 2033152 | tf_op jit(solution)/shard_map/dot_general | solution.py:468
  114.2 7.4 %mp_gather_sum.2 = (bf16[128,1024]{1,0:T(8,128)(2,1)S(1)}, f32[8,128]{1,0:T(8,128)S(1)}) custom-call(bf16[128,256]{1,0:T(8,128)(2,1)S(1)} %get-tuple-element.35.own_ref, f32[8,128]{1,0:T(8,128)S(1)} %broadcast_in_dim.105.term_ref), custom_call_target="tpu_custom_call" | custom-call | bytes 327680 | tf_op jit(solution)/shard_map/mp_gather_sum/pallas_call | solution.py:292
  121.7 3.4 %convolution_convert_fusion.3.part_ref = bf16[128,1024]{1,0:T(8,128)(2,1)S(1)} fusion(bf16[1024,1024]{1,0:T(8,128)(2,1)S(1)} %copy-done, bf16[1024,1024]{1,0:T(8,128)(2,1)} %param.11, f32[128,1024]{1,0:T(8,128)} %copy-done.8, bf16[128,1024]{1,0:T(8,128)(2,1)S(1)} %get-tuple-element.12, f32[128]{0:T(128)S(1)} %bitcast_multiply_fusion.5, ...), kind=kOutput, calls=%fused_computation.11 | convolution fusion | flops 539099136 | bytes 5506048 | tf_op jit(solution)/shard_map/dot_general | solution.py:377
  125.1 7.4 %mp_scatter.4 = f32[128,256]{1,0:T(8,128)S(1)} custom-call(bf16[128,1024]{1,0:T(8,128)(2,1)S(1)} %convolution_convert_fusion.3.part_ref), custom_call_target="tpu_custom_call" | custom-call | flops 131072 | bytes 524288 | tf_op jit(solution)/shard_map/mp_scatter/pallas_call | solution.py:262
  132.8 1.6 add_convert_fusion.1
  134.4 20.6 %all-to-all-done = bf16[128,16,256]{2,1,0:T(8,128)(2,1)} async-done(((bf16[128,16,256]{2,1,0:T(8,128)(2,1)}), bf16[128,16,256]{2,1,0:T(8,128)(2,1)}, u32[]{:S(2)}, u32[]{:S(2)}) %all-to-all-start) | async-done | bytes 1048608 | tf_op jit(solution)/shard_map/all_to_all | solution.py:464
  155.0 2.1 %multiply_reduce_fusion.1 = (f32[128]{0:T(128)S(1)}, bf16[128,256]{1,0:T(8,128)(2,1)S(1)}, f32[128,256]{1,0:T(8,128)S(1)}) fusion(f32[128,256]{1,0:T(8,128)S(1)} %get-tuple-element.29, f32[128]{0:T(128)S(1)} %copy-done.14, bf16[2048,256]{1,0:T(8,128)(2,1)} %bitcast.12, s32[2048]{0:T(1024)S(1)} %eq.63, f32[128,256]{1,0:T(8,128)S(1)} %copy-done.6, ...), kind=kOutput, calls=%fused_computation.62 | convolution fusion | flops 134676352 | bytes 1517056 | tf_op jit(solution)/shard_map/dot_general | solution.py:475
  157.1 8.4 %mp_gather_sum.3 = (bf16[128,1024]{1,0:T(8,128)(2,1)S(1)}, f32[8,128]{1,0:T(8,128)S(1)}) custom-call(bf16[128,256]{1,0:T(8,128)(2,1)S(1)} %get-tuple-element.33.own_ref, f32[8,128]{1,0:T(8,128)S(1)} %broadcast_in_dim.106.term_ref), custom_call_target="tpu_custom_call" | custom-call | bytes 327680 | tf_op jit(solution)/shard_map/mp_gather_sum/pallas_call | solution.py:292
  165.5 3.2 %convolution_convert_fusion.2.part_ref = bf16[128,1024]{1,0:T(8,128)(2,1)S(1)} fusion(bf16[1024,1024]{1,0:T(8,128)(2,1)S(1)} %copy-done, bf16[1024,1024]{1,0:T(8,128)(2,1)} %param.11, f32[128,1024]{1,0:T(8,128)} %copy-done.7, bf16[128,1024]{1,0:T(8,128)(2,1)S(1)} %get-tuple-element.16, f32[128]{0:T(128)S(1)} %bitcast_multiply_fusion.2, ...), kind=kOutput, calls=%fused_computation.10 | convolution fusion | flops 539099136 | bytes 5506048 | tf_op jit(solution)/shard_map/dot_general | solution.py:377
  168.7 7.3 %mp_scatter.5 = f32[128,256]{1,0:T(8,128)S(1)} custom-call(bf16[128,1024]{1,0:T(8,128)(2,1)S(1)} %convolution_convert_fusion.2.part_ref), custom_call_target="tpu_custom_call" | custom-call | flops 131072 | bytes 524288 | tf_op jit(solution)/shard_map/mp_scatter/pallas_call | solution.py:262
  176.0 0.7 add_convert_fusion
  (63 shorter events, 3.4 us)
Async XLA Ops:
  0.6 1.6 copy-start
  2.2 2.3 %copy-start.3 = (bf16[1024,1024]{1,0:T(8,128)(2,1)S(1)}, bf16[1024,1024]{1,0:T(8,128)(2,1)}, u32[]{:S(2)}) copy-start(bf16[1024,1024]{1,0:T(8,128)(2,1)} %param.11) | copy-start | bytes 6291460
  3.8 0.8 copy-start.7
  4.6 10.0 %copy-start.12 = (s32[1,128,16]{1,2,0:T(8,128)S(1)}, s32[1,128,16]{1,2,0:T(8,128)}, u32[]{:S(2)}) copy-start(s32[1,128,16]{1,2,0:T(8,128)} %param.14) | copy-start | bytes 24580
  4.6 10.2 %copy-start.10 = (bf16[128,1024]{1,0:T(8,128)(2,1)S(1)}, bf16[128,1024]{1,0:T(8,128)(2,1)}, u32[]{:S(2)}) copy-start(bf16[128,1024]{1,0:T(8,128)(2,1)} %param.8) | copy-start | bytes 786436
  14.6 2.6 %copy-start.9 = (bf16[128,256]{1,0:T(8,128)(2,1)}, bf16[128,256]{1,0:T(8,128)(2,1)S(1)}, u32[]{:S(2)}) copy-start(bf16[128,256]{1,0:T(8,128)(2,1)S(1)} %convert_element_type.125) | copy-start | bytes 196612
  14.8 1.8 %copy-start.4 = (bf16[1024,1024]{1,0:T(8,128)(2,1)S(1)}, bf16[1024,1024]{1,0:T(8,128)(2,1)}, u32[]{:S(2)}) copy-start(bf16[1024,1024]{1,0:T(8,128)(2,1)} %param.11) | copy-start | bytes 6291460
  15.3 0.8 copy-start.8
  55.7 17.3 %copy-start.11 = (s32[128,8]{0,1:T(8,128)S(1)}, s32[128,8]{0,1:T(8,128)}, u32[]{:S(2)}) copy-start(s32[128,8]{0,1:T(8,128)} %param.12) | copy-start | bytes 12292
  72.4 39.8 %copy-start.5 = (f32[128,256]{1,0:T(8,128)}, f32[128,256]{1,0:T(8,128)S(1)}, u32[]{:S(2)}) copy-start(f32[128,256]{1,0:T(8,128)S(1)} %get-tuple-element.27) | copy-start | bytes 393220
  72.6 11.3 %copy-start.16 = (s32[128,8]{0,1:T(8,128)S(1)}, s32[128,8]{0,1:T(8,128)}, u32[]{:S(2)}) copy-start(s32[128,8]{0,1:T(8,128)} %param.13) | copy-start | bytes 12292
  89.0 66.0 %all-to-all-start = ((bf16[128,16,256]{2,1,0:T(8,128)(2,1)}), bf16[128,16,256]{2,1,0:T(8,128)(2,1)}, u32[]{:S(2)}, u32[]{:S(2)}) async-start(bf16[128,16,256]{2,1,0:T(8,128)(2,1)} %bitcast.70), calls=%async_computation | async-start | bytes 2097152 | tf_op jit(solution)/shard_map/all_to_all | solution.py:464
  111.6 2.6 %copy-start.1 = (bf16[256,1024]{1,0:T(8,128)(2,1)}, bf16[256,1024]{1,0:T(8,128)(2,1)S(1)}, u32[]{:S(2)}) copy-start(bf16[256,1024]{1,0:T(8,128)(2,1)S(1)} %mp_gather.1) | copy-start | bytes 1572868
  121.7 10.9 %copy-start.13 = (s32[1,128,16]{1,2,0:T(8,128)S(1)}, s32[1,128,16]{1,2,0:T(8,128)}, u32[]{:S(2)}) copy-start(s32[1,128,16]{1,2,0:T(8,128)} %param.14) | copy-start | bytes 24580
  121.7 11.1 %copy-start.6 = (f32[128,256]{1,0:T(8,128)S(1)}, f32[128,256]{1,0:T(8,128)}, u32[]{:S(2)}) copy-start(f32[128,256]{1,0:T(8,128)} %copy-done.5) | copy-start | bytes 393220
  121.7 33.3 %copy-start.14 = (f32[128]{0:T(128)S(1)}, f32[128]{0:T(128)}, u32[]{:S(2)}) copy-start(f32[128]{0:T(128)} %get-tuple-element.36) | copy-start | bytes 1540
  121.7 33.3 %copy-start.17 = (f32[128]{0:T(128)S(1)}, f32[128]{0:T(128)}, u32[]{:S(2)}) copy-start(f32[128]{0:T(128)} %get-tuple-element.22) | copy-start | bytes 1540
  125.1 40.3 %copy-start.2 = (bf16[256,1024]{1,0:T(8,128)(2,1)S(1)}, bf16[256,1024]{1,0:T(8,128)(2,1)}, u32[]{:S(2)}) copy-start(bf16[256,1024]{1,0:T(8,128)(2,1)} %copy-done.1) | copy-start | bytes 1572868
  132.6 32.9 %copy-start.15 = (f32[128]{0:T(128)S(1)}, f32[128]{0:T(128)}, u32[]{:S(2)}) copy-start(f32[128]{0:T(128)} %get-tuple-element.36) | copy-start | bytes 1540

commit v5 on v4

--- a/solution.py
+++ b/solution.py
@@ -407,7 +407,7 @@
         axis=0,
     )
     pre_query, part_query = encode_part(query_states, w_in, w_out)
-    column, sum_query = column_gather(block, part_query, plane, 3, 7)
+    column, sum_query = column_gather(block, part_query, plane, 9, 7)
     out_query = own_columns(query_states).astype(jnp.float32) + sum_query
     start = (lax.axis_index("dp") // plane) * plane * capacity
     served_here = lax.dynamic_slice(
@@ -461,10 +461,11 @@
     outgoing_grad = lax.dot_general(
         slot_grad.astype(jnp.bfloat16), half_query, (((0,), (0,)), ((), ())), preferred_element_type=jnp.float32
     ).astype(jnp.bfloat16)
+    late_weight, outgoing_grad = lax.optimization_barrier((grad_neg * inv_neg, outgoing_grad))
     returned = lax.all_to_all(
         outgoing_grad.reshape(owners, capacity, column_width), "dp", split_axis=0, concat_axis=0, tiled=True
     ).reshape(slots, column_width)
-    slot_weight = jnp.sum(jnp.where(slot_hit, (grad_neg * inv_neg)[:, :, None], 0.0), axis=0)
+    slot_weight = jnp.sum(jnp.where(slot_hit, late_weight[:, :, None], 0.0), axis=0)
     grad_query_emb = (grad_pos * inv_pass)[:, None] * out_pass + jnp.dot(
         slot_weight.astype(jnp.bfloat16), slot_rows, preferred_element_type=jnp.float32
     )

time: 178 us -> 178 us (level)
  no operation moved by 1% of the time
where the time goes in v5:
time: 178 us; the launch traced here: 177 us
  Pallas kernels  110 us (62%)
  waiting for transfers between devices  19.5 us (11%)
  matrix products  15.4 us (9%)
  other arithmetic  13.2 us (7%)
  starting transfers between devices  12.3 us (7%)
  local copies, waits for them, and re-layouts  5.03 us (3%)
  between operations  1.82 us (1%)
    pallas_call x1, Pallas kernels, column_gather(): pl.pallas_call(functools.partial(column_kernel, ways, plane, parts), out_...  38.8 us
    pallas_call x3, Pallas kernels, mp_scatter(): pl.pallas_call(functools.partial(scatter_kernel, ways), out_shape=jax.Sha...  23.2 us
    all_to_all x1, waiting for transfers between devices, shards(): lax.all_to_all(outgoing_grad.reshape(owners, capacity, column_width), 'dp...  19.5 us
    pallas_call x1, Pallas kernels, plane_exchange(): pl.pallas_call(functools.partial(plane_kernel, plane, capacity), out_shap...  15.8 us
    pallas_call x2, Pallas kernels, mp_gather_sum(): pl.pallas_call(functools.partial(gather_sum_kernel, ways), out_shape=(jax...  15.7 us
    all_to_all x1, starting transfers between devices, shards(): lax.all_to_all(outgoing_grad.reshape(owners, capacity, column_width), 'dp...  12.3 us
    pallas_call x1, Pallas kernels, mp_gather(): pl.pallas_call(functools.partial(gather_kernel, ways), out_shape=jax.Shap...  10.6 us
    dot_general x2, matrix products, decode(): lax.dot_general(grad_pre, w_in, contract, preferred_element_type=jnp.floa...  6.63 us
  transfers between devices with their start and end apart: 1, of which 1 were waited for; matrix products, arithmetic and copies ran while one was open for 5% of the time, Pallas kernels for 14%

profile of v5, /device:TPU:32, one launch (start us, length us, event | category | flops | bytes accessed | tf_op | source)
XLA Modules:
  0.0 177.5 jit_solution(3098252438945874812)
XLA Ops:
  0.7 1.5 copy-done
  2.2 1.5 fusion.56
  3.8 0.8 copy-done.7
  5.1 8.5 %mp_scatter.3 = f32[128,256]{1,0:T(8,128)S(1)} custom-call(bf16[128,1024]{1,0:T(8,128)(2,1)S(1)} %convolution_convert_fusion.5.part_ref), custom_call_target="tpu_custom_call" | custom-call | flops 131072 | bytes 524288 | tf_op jit(solution)/shard_map/mp_scatter/pallas_call | solution.py:262
  13.6 1.0 multiply_reduce_fusion.4
  15.3 0.8 copy-done.8
  17.3 38.8 %column_gather.1 = (bf16[16,144,256]{2,1,0:T(8,128)(2,1)S(1)}, f32[128,256]{1,0:T(8,128)S(1)}) custom-call(bf16[144,256]{1,0:T(8,128)(2,1)S(1)} %maximum_maximum_fusion.block_ref, bf16[128,1024]{1,0:T(8,128)(2,1)S(1)} %convolution_convert_fusion.4.part_ref), custom_call_target="tpu_custom_call" | custom-call | tf_op jit(solution)/shard_map/column_gather/pallas_call | solution.py:327
  56.1 0.7 convolution_convert_fusion.1.rows_ref
  56.9 15.8 %plane_exchange.1 = bf16[16,128,256]{2,1,0:T(8,128)(2,1)S(1)} custom-call(bf16[16,128,256]{2,1,0:T(8,128)(2,1)S(1)} %convolution_convert_fusion.1.rows_ref), custom_call_target="tpu_custom_call" | custom-call | tf_op jit(solution)/shard_map/plane_exchange/pallas_call | solution.py:345
  72.7 1.0 multiply_reduce_fusion.3
  75.3 2.8 %select_reduce_fusion.2 = (f32[8,128]{1,0:T(8,128)S(1)}, f32[8,128]{1,0:T(8,128)S(1)}) fusion(f32[2048]{0:T(1024)S(1)} %bitcast.73, s32[8,128]{1,0:T(8,128)S(1)} %convert_add_fusion.2, f32[128,2048]{1,0:T(8,128)S(1)} %fusion.58), kind=kLoop, calls=%fused_computation.2 | loop fusion | flops 10483712 | bytes 1069056 | tf_op jit(solution)/shard_map/reduce_sum | solution.py:442
  78.2 6.1 %mp_sum.1 = f32[24,128]{1,0:T(8,128)S(1)} custom-call(f32[24,128]{1,0:T(8,128)S(1)} %concatenate.10.term_ref), custom_call_target="tpu_custom_call" | custom-call | bytes 61440 | tf_op jit(solution)/shard_map/mp_sum/pallas_call | solution.py:309
  85.0 0.6 fusion.54
  85.6 1.4 select_reduce_fusion.1
  87.0 1.5 convolution_convert_fusion
  88.5 12.3 %all-to-all-start = ((bf16[128,16,256]{2,1,0:T(8,128)(2,1)}), bf16[128,16,256]{2,1,0:T(8,128)(2,1)}, u32[]{:S(2)}, u32[]{:S(2)}) async-start(bf16[128,16,256]{2,1,0:T(8,128)(2,1)} %bitcast.70), calls=%async_computation | async-start | bytes 2097152 | tf_op jit(solution)/shard_map/all_to_all | solution.py:465
  100.8 0.9 pad_maximum_fusion.own_ref
  101.6 10.6 %mp_gather.1 = bf16[256,1024]{1,0:T(8,128)(2,1)S(1)} custom-call(bf16[256,256]{1,0:T(8,128)(2,1)S(1)} %pad_maximum_fusion.own_ref), custom_call_target="tpu_custom_call" | custom-call | bytes 655360 | tf_op jit(solution)/shard_map/mp_gather/pallas_call | solution.py:277
  112.3 0.8 copy-done.1
  113.0 0.5 bitcast_multiply_fusion.4
  113.6 1.4 select_reduce_fusion
  115.0 1.0 multiply_reduce_fusion.2
  116.0 7.4 %mp_gather_sum.2 = (bf16[128,1024]{1,0:T(8,128)(2,1)S(1)}, f32[8,128]{1,0:T(8,128)S(1)}) custom-call(bf16[128,256]{1,0:T(8,128)(2,1)S(1)} %get-tuple-element.37.own_ref, f32[8,128]{1,0:T(8,128)S(1)} %broadcast_in_dim.105.term_ref), custom_call_target="tpu_custom_call" | custom-call | bytes 327680 | tf_op jit(solution)/shard_map/mp_gather_sum/pallas_call | solution.py:292
  123.4 3.4 %convolution_convert_fusion.3.part_ref = bf16[128,1024]{1,0:T(8,128)(2,1)S(1)} fusion(bf16[1024,1024]{1,0:T(8,128)(2,1)S(1)} %copy-done, bf16[1024,1024]{1,0:T(8,128)(2,1)} %param.11, f32[128,1024]{1,0:T(8,128)} %copy-done.8, bf16[128,1024]{1,0:T(8,128)(2,1)S(1)} %get-tuple-element.16, f32[128]{0:T(128)S(1)} %bitcast_multiply_fusion.5, ...), kind=kOutput, calls=%fused_computation.11 | convolution fusion | flops 539099136 | bytes 5506048 | tf_op jit(solution)/shard_map/dot_general | solution.py:377
  126.8 7.4 %mp_scatter.4 = f32[128,256]{1,0:T(8,128)S(1)} custom-call(bf16[128,1024]{1,0:T(8,128)(2,1)S(1)} %convolution_convert_fusion.3.part_ref), custom_call_target="tpu_custom_call" | custom-call | flops 131072 | bytes 524288 | tf_op jit(solution)/shard_map/mp_scatter/pallas_call | solution.py:262
  134.5 1.6 add_convert_fusion.1
  136.1 19.5 %all-to-all-done = bf16[128,16,256]{2,1,0:T(8,128)(2,1)} async-done(((bf16[128,16,256]{2,1,0:T(8,128)(2,1)}), bf16[128,16,256]{2,1,0:T(8,128)(2,1)}, u32[]{:S(2)}, u32[]{:S(2)}) %all-to-all-start) | async-done | bytes 1048608 | tf_op jit(solution)/shard_map/all_to_all | solution.py:465
  155.7 2.1 %multiply_reduce_fusion.1 = (f32[128]{0:T(128)S(1)}, bf16[128,256]{1,0:T(8,128)(2,1)S(1)}, f32[128,256]{1,0:T(8,128)S(1)}) fusion(f32[128,256]{1,0:T(8,128)S(1)} %get-tuple-element.31, f32[128]{0:T(128)S(1)} %copy-done.14, bf16[2048,256]{1,0:T(8,128)(2,1)} %bitcast.12, s32[2048]{0:T(1024)S(1)} %eq.63, f32[128,256]{1,0:T(8,128)S(1)} %copy-done.6, ...), kind=kOutput, calls=%fused_computation.62 | convolution fusion | flops 134676352 | bytes 1517056 | tf_op jit(solution)/shard_map/dot_general | solution.py:476
  157.7 8.4 %mp_gather_sum.3 = (bf16[128,1024]{1,0:T(8,128)(2,1)S(1)}, f32[8,128]{1,0:T(8,128)S(1)}) custom-call(bf16[128,256]{1,0:T(8,128)(2,1)S(1)} %get-tuple-element.35.own_ref, f32[8,128]{1,0:T(8,128)S(1)} %broadcast_in_dim.106.term_ref), custom_call_target="tpu_custom_call" | custom-call | bytes 327680 | tf_op jit(solution)/shard_map/mp_gather_sum/pallas_call | solution.py:292
  166.1 3.2 %convolution_convert_fusion.2.part_ref = bf16[128,1024]{1,0:T(8,128)(2,1)S(1)} fusion(bf16[1024,1024]{1,0:T(8,128)(2,1)S(1)} %copy-done, bf16[1024,1024]{1,0:T(8,128)(2,1)} %param.11, f32[128,1024]{1,0:T(8,128)} %copy-done.7, bf16[128,1024]{1,0:T(8,128)(2,1)S(1)} %get-tuple-element.20, f32[128]{0:T(128)S(1)} %bitcast_multiply_fusion.2, ...), kind=kOutput, calls=%fused_computation.10 | convolution fusion | flops 539099136 | bytes 5506048 | tf_op jit(solution)/shard_map/dot_general | solution.py:377
  169.4 7.3 %mp_scatter.5 = f32[128,256]{1,0:T(8,128)S(1)} custom-call(bf16[128,1024]{1,0:T(8,128)(2,1)S(1)} %convolution_convert_fusion.2.part_ref), custom_call_target="tpu_custom_call" | custom-call | flops 131072 | bytes 524288 | tf_op jit(solution)/shard_map/mp_scatter/pallas_call | solution.py:262
  176.7 0.7 add_convert_fusion
  (64 shorter events, 4.4 us)
Async XLA Ops:
  0.6 1.6 copy-start
  2.2 2.3 %copy-start.3 = (bf16[1024,1024]{1,0:T(8,128)(2,1)S(1)}, bf16[1024,1024]{1,0:T(8,128)(2,1)}, u32[]{:S(2)}) copy-start(bf16[1024,1024]{1,0:T(8,128)(2,1)} %param.11) | copy-start | bytes 6291460
  3.8 0.8 copy-start.7
  4.6 10.0 %copy-start.12 = (s32[1,128,16]{1,2,0:T(8,128)S(1)}, s32[1,128,16]{1,2,0:T(8,128)}, u32[]{:S(2)}) copy-start(s32[1,128,16]{1,2,0:T(8,128)} %param.14) | copy-start | bytes 24580
  4.6 10.2 %copy-start.10 = (bf16[128,1024]{1,0:T(8,128)(2,1)S(1)}, bf16[128,1024]{1,0:T(8,128)(2,1)}, u32[]{:S(2)}) copy-start(bf16[128,1024]{1,0:T(8,128)(2,1)} %param.8) | copy-start | bytes 786436
  14.6 2.6 %copy-start.9 = (bf16[128,256]{1,0:T(8,128)(2,1)}, bf16[128,256]{1,0:T(8,128)(2,1)S(1)}, u32[]{:S(2)}) copy-start(bf16[128,256]{1,0:T(8,128)(2,1)S(1)} %convert_element_type.125) | copy-start | bytes 196612
  14.8 1.8 %copy-start.4 = (bf16[1024,1024]{1,0:T(8,128)(2,1)S(1)}, bf16[1024,1024]{1,0:T(8,128)(2,1)}, u32[]{:S(2)}) copy-start(bf16[1024,1024]{1,0:T(8,128)(2,1)} %param.11) | copy-start | bytes 6291460
  15.3 0.8 copy-start.8
  56.9 17.2 %copy-start.11 = (s32[128,8]{0,1:T(8,128)S(1)}, s32[128,8]{0,1:T(8,128)}, u32[]{:S(2)}) copy-start(s32[128,8]{0,1:T(8,128)} %param.12) | copy-start | bytes 12292
  73.6 41.4 %copy-start.5 = (f32[128,256]{1,0:T(8,128)}, f32[128,256]{1,0:T(8,128)S(1)}, u32[]{:S(2)}) copy-start(f32[128,256]{1,0:T(8,128)S(1)} %get-tuple-element.29) | copy-start | bytes 393220
  73.7 11.2 %copy-start.16 = (s32[128,8]{0,1:T(8,128)S(1)}, s32[128,8]{0,1:T(8,128)}, u32[]{:S(2)}) copy-start(s32[128,8]{0,1:T(8,128)} %param.13) | copy-start | bytes 12292
  88.5 67.2 %all-to-all-start = ((bf16[128,16,256]{2,1,0:T(8,128)(2,1)}), bf16[128,16,256]{2,1,0:T(8,128)(2,1)}, u32[]{:S(2)}, u32[]{:S(2)}) async-start(bf16[128,16,256]{2,1,0:T(8,128)(2,1)} %bitcast.70), calls=%async_computation | async-start | bytes 2097152 | tf_op jit(solution)/shard_map/all_to_all | solution.py:465
  112.2 0.8 copy-start.1
  123.4 10.9 %copy-start.13 = (s32[1,128,16]{1,2,0:T(8,128)S(1)}, s32[1,128,16]{1,2,0:T(8,128)}, u32[]{:S(2)}) copy-start(s32[1,128,16]{1,2,0:T(8,128)} %param.14) | copy-start | bytes 24580
  123.4 11.1 %copy-start.6 = (f32[128,256]{1,0:T(8,128)S(1)}, f32[128,256]{1,0:T(8,128)}, u32[]{:S(2)}) copy-start(f32[128,256]{1,0:T(8,128)} %copy-done.5) | copy-start | bytes 393220
  123.4 32.2 %copy-start.14 = (f32[128]{0:T(128)S(1)}, f32[128]{0:T(128)}, u32[]{:S(2)}) copy-start(f32[128]{0:T(128)} %get-tuple-element.38) | copy-start | bytes 1540
  123.4 32.2 %copy-start.17 = (f32[128]{0:T(128)S(1)}, f32[128]{0:T(128)}, u32[]{:S(2)}) copy-start(f32[128]{0:T(128)} %get-tuple-element.24) | copy-start | bytes 1540
  126.8 39.3 %copy-start.2 = (bf16[256,1024]{1,0:T(8,128)(2,1)S(1)}, bf16[256,1024]{1,0:T(8,128)(2,1)}, u32[]{:S(2)}) copy-start(bf16[256,1024]{1,0:T(8,128)(2,1)} %copy-done.1) | copy-start | bytes 1572868
  134.3 31.9 %copy-start.15 = (f32[128]{0:T(128)S(1)}, f32[128]{0:T(128)}, u32[]{:S(2)}) copy-start(f32[128]{0:T(128)} %get-tuple-element.38) | copy-start | bytes 1540

commit v6 on v4

--- a/solution.py
+++ b/solution.py
@@ -212,36 +212,84 @@
         copy.wait_send()
 
 
-def plane_kernel(plane, capacity, rows_ref, out_ref, send_sem, recv_sem):
+def plane_kernel(plane, capacity, rows_ref, out_ref, held, send_sem, recv_sem, out_send, out_recv, on_send, on_recv):
     place = lax.axis_index("dp")
     here = lax.rem(place, plane)
     base = place - here
-    barrier = pltpu.get_barrier_semaphore()
-    for step in range(1, plane):
-        pl.semaphore_signal(
-            barrier,
-            inc=1,
-            device_id={"dp": base + lax.rem(here + step, plane)},
-            device_id_type=pl.DeviceIdType.MESH,
-        )
-    pl.semaphore_wait(barrier, plane - 1)
-    own = pl.ds(pl.multiple_of(here * capacity, capacity), capacity)
-    copies = []
-    for step in range(1, plane):
-        peer = lax.rem(here + step, plane)
-        copy = pltpu.make_async_remote_copy(
-            src_ref=rows_ref.at[:, pl.ds(pl.multiple_of(peer * capacity, capacity), capacity)],
-            dst_ref=out_ref.at[:, own],
-            send_sem=send_sem.at[step - 1],
-            recv_sem=recv_sem.at[step - 1],
+    chips, half = plane // 2, rows_ref.shape[0] // 2
+    chip, core = here // 2, lax.rem(here, 2)
+
+    def at(chip_step, core_index):
+        return lax.rem(chip + chip_step, chips) * 2 + core_index
+
+    def span(index):
+        return pl.ds(pl.multiple_of(index * capacity, capacity), capacity)
+
+    def copy_to(source, target, send, recv, peer):
+        return pltpu.make_async_remote_copy(
+            src_ref=source,
+            dst_ref=target,
+            send_sem=send,
+            recv_sem=recv,
             device_id={"dp": base + peer},
             device_id_type=pl.DeviceIdType.MESH,
         )
+
+    near = [at(1, core), at(1, 1 - core), at(chips - 1, core), at(chips - 1, 1 - core), at(0, 1 - core)]
+    barrier = pltpu.get_barrier_semaphore()
+    for peer in near:
+        pl.semaphore_signal(barrier, inc=1, device_id={"dp": base + peer}, device_id_type=pl.DeviceIdType.MESH)
+    pl.semaphore_wait(barrier, len(near))
+    ways = (1, chips - 1)
+    first = []
+    for which, way in enumerate(ways):
+        for target_core in range(2):
+            slot = which * 2 + target_core
+            copy = copy_to(
+                rows_ref.at[pl.ds(which * half, half), span(at(2, target_core))],
+                held.at[slot],
+                out_send.at[slot],
+                out_recv.at[slot],
+                at(way, core),
+            )
+            copy.start()
+            first.append(copy)
+    copies = []
+    for step, peer in enumerate(near):
+        copy = copy_to(
+            rows_ref.at[:, span(peer)], out_ref.at[:, span(here)], send_sem.at[step], recv_sem.at[step], peer
+        )
         copy.start()
         copies.append(copy)
-    out_ref[:, own] = rows_ref[:, own]
+    out_ref[:, span(here)] = rows_ref[:, span(here)]
+    second = []
+    for which, way in enumerate(ways):
+        for target_core in range(2):
+            slot = which * 2 + target_core
+            first[slot].wait_recv()
+            copy = copy_to(
+                held.at[slot],
+                out_ref.at[pl.ds(which * half, half), span(at(chips - way, core))],
+                on_send.at[slot],
+                on_recv.at[which * 2 + core],
+                at(way, target_core),
+            )
+            copy.start()
+            second.append(copy)
     for copy in copies:
         copy.wait()
+    for which, way in enumerate(ways):
+        for source_core in range(2):
+            slot = which * 2 + source_core
+            copy_to(
+                held.at[slot],
+                out_ref.at[pl.ds(which * half, half), span(at(2, source_core))],
+                on_send.at[slot],
+                on_recv.at[slot],
+                at(way, source_core),
+            ).wait_recv()
+    for copy in first + second:
+        copy.wait_send()
 
 
 def in_vmem(count):
@@ -347,7 +395,8 @@
         out_shape=jax.ShapeDtypeStruct(rows.shape, rows.dtype),
         in_specs=in_vmem(1),
         out_specs=pl.BlockSpec(memory_space=pltpu.VMEM),
-        scratch_shapes=[sem((plane - 1,)), sem((plane - 1,))],
+        scratch_shapes=[pltpu.VMEM((4, rows.shape[0] // 2, capacity, rows.shape[2]), rows.dtype)]
+        + [sem((5,)), sem((5,)), sem((4,)), sem((4,)), sem((4,)), sem((4,))],
         compiler_params=params(number),
         name="plane_exchange",
     )(rows)

time: 178 us -> 178 us (level)
  no operation moved by 1% of the time
where the time goes in v6:
time: 178 us; the launch traced here: 177 us
  Pallas kernels  109 us (61%)
  waiting for transfers between devices  20.5 us (12%)
  matrix products  16.4 us (9%)
  other arithmetic  13.5 us (8%)
  starting transfers between devices  11.2 us (6%)
  local copies, waits for them, and re-layouts  4.25 us (2%)
  between operations  1.8 us (1%)
    pallas_call x1, Pallas kernels, column_gather(): pl.pallas_call(functools.partial(column_kernel, ways, plane, parts), out_...  37.6 us
    pallas_call x3, Pallas kernels, mp_scatter(): pl.pallas_call(functools.partial(scatter_kernel, ways), out_shape=jax.Sha...  23.2 us
    all_to_all x1, waiting for transfers between devices, shards(): lax.all_to_all(outgoing_grad.reshape(owners, capacity, column_width), 'dp...  20.5 us
    pallas_call x1, Pallas kernels, plane_exchange(): pl.pallas_call(functools.partial(plane_kernel, plane, capacity), out_shap...  16.1 us
    pallas_call x2, Pallas kernels, mp_gather_sum(): pl.pallas_call(functools.partial(gather_sum_kernel, ways), out_shape=(jax...  15.9 us
    all_to_all x1, starting transfers between devices, shards(): lax.all_to_all(outgoing_grad.reshape(owners, capacity, column_width), 'dp...  11.2 us
    pallas_call x1, Pallas kernels, mp_gather(): pl.pallas_call(functools.partial(gather_kernel, ways), out_shape=jax.Shap...  10.6 us
    dot_general x2, matrix products, decode(): lax.dot_general(grad_pre, w_in, contract, preferred_element_type=jnp.floa...  6.62 us
  transfers between devices with their start and end apart: 1, of which 1 were waited for; matrix products, arithmetic and copies ran while one was open for 5% of the time, Pallas kernels for 14%

profile of v6, /device:TPU:32, one launch (start us, length us, event | category | flops | bytes accessed | tf_op | source)
XLA Modules:
  0.0 177.1 jit_solution(152028104691424013)
XLA Ops:
  0.7 1.5 copy-done
  2.2 1.5 fusion.56
  3.8 0.8 copy-done.7
  5.1 8.5 %mp_scatter.3 = f32[128,256]{1,0:T(8,128)S(1)} custom-call(bf16[128,1024]{1,0:T(8,128)(2,1)S(1)} %convolution_convert_fusion.5.part_ref), custom_call_target="tpu_custom_call" | custom-call | flops 131072 | bytes 524288 | tf_op jit(solution)/shard_map/mp_scatter/pallas_call | solution.py:310
  13.6 1.0 multiply_reduce_fusion.4
  15.3 0.8 copy-done.8
  16.1 0.5 copy-done.4
  17.3 37.6 %column_gather.1 = (bf16[16,144,256]{2,1,0:T(8,128)(2,1)S(1)}, f32[128,256]{1,0:T(8,128)S(1)}) custom-call(bf16[144,256]{1,0:T(8,128)(2,1)S(1)} %maximum_maximum_fusion.block_ref, bf16[128,1024]{1,0:T(8,128)(2,1)S(1)} %convolution_convert_fusion.4.part_ref), custom_call_target="tpu_custom_call" | custom-call | tf_op jit(solution)/shard_map/column_gather/pallas_call | solution.py:375
  54.9 0.7 convolution_convert_fusion.1.rows_ref
  55.7 16.1 %plane_exchange.1 = bf16[16,128,256]{2,1,0:T(8,128)(2,1)S(1)} custom-call(bf16[16,128,256]{2,1,0:T(8,128)(2,1)S(1)} %convolution_convert_fusion.1.rows_ref), custom_call_target="tpu_custom_call" | custom-call | tf_op jit(solution)/shard_map/plane_exchange/pallas_call | solution.py:393
  71.8 1.0 multiply_reduce_fusion.3
  73.9 0.5 fusion.58
  74.4 2.8 %select_reduce_fusion.2 = (f32[8,128]{1,0:T(8,128)S(1)}, f32[8,128]{1,0:T(8,128)S(1)}) fusion(f32[2048]{0:T(1024)S(1)} %bitcast.73, s32[8,128]{1,0:T(8,128)S(1)} %convert_add_fusion.2, f32[128,2048]{1,0:T(8,128)S(1)} %fusion.58), kind=kLoop, calls=%fused_computation.2 | loop fusion | flops 10483712 | bytes 1069056 | tf_op jit(solution)/shard_map/reduce_sum | solution.py:491
  77.3 6.1 %mp_sum.1 = f32[24,128]{1,0:T(8,128)S(1)} custom-call(f32[24,128]{1,0:T(8,128)S(1)} %concatenate.10.term_ref), custom_call_target="tpu_custom_call" | custom-call | bytes 61440 | tf_op jit(solution)/shard_map/mp_sum/pallas_call | solution.py:357
  84.1 0.5 fusion.54
  84.7 3.1 %select_reduce_fusion = (bf16[128,2048]{1,0:T(8,128)(2,1)}, bf16[128,2048]{1,0:T(8,128)(2,1)S(1)}) fusion(f32[8,128]{1,0:T(8,128)S(1)} %get-tuple-element.39, s32[8,128]{1,0:T(8,128)S(1)} %convert_add_fusion.2, f32[8,128]{1,0:T(8,128)S(1)} %get-tuple-element.38), kind=kLoop, calls=%fused_computation | loop fusion | flops 9961472 | bytes 1060864 | tf_op jit(solution)/shard_map/reduce_sum | solution.py:516
  87.8 1.5 convolution_convert_fusion
  89.3 11.2 %all-to-all-start = ((bf16[128,16,256]{2,1,0:T(8,128)(2,1)}), bf16[128,16,256]{2,1,0:T(8,128)(2,1)}, u32[]{:S(2)}, u32[]{:S(2)}) async-start(bf16[128,16,256]{2,1,0:T(8,128)(2,1)} %bitcast.70), calls=%async_computation | async-start | bytes 2097152 | tf_op jit(solution)/shard_map/all_to_all | solution.py:513
  100.5 0.9 pad_maximum_fusion.own_ref
  101.3 10.6 %mp_gather.1 = bf16[256,1024]{1,0:T(8,128)(2,1)S(1)} custom-call(bf16[256,256]{1,0:T(8,128)(2,1)S(1)} %pad_maximum_fusion.own_ref), custom_call_target="tpu_custom_call" | custom-call | bytes 655360 | tf_op jit(solution)/shard_map/mp_gather/pallas_call | solution.py:325
  111.9 0.6 bitcast_multiply_fusion.4
  112.6 2.0 %multiply_reduce_fusion.2 = (f32[128]{0:T(128)S(1)}, bf16[128,256]{1,0:T(8,128)(2,1)S(1)}, f32[128,256]{1,0:T(8,128)}) fusion(f32[128,256]{1,0:T(8,128)S(1)} %get-tuple-element.27, f32[128]{0:T(128)S(1)} %fusion.53, bf16[128,2048]{1,0:T(8,128)(2,1)} %get-tuple-element.18, bf16[2048,256]{1,0:T(8,128)(2,1)S(1)} %bitcast.69, ...), kind=kOutput, calls=%fused_computation.64 | convolution fusion | flops 134414208 | bytes 2033152 | tf_op jit(solution)/shard_map/dot_general | solution.py:517
  114.6 7.5 %mp_gather_sum.2 = (bf16[128,1024]{1,0:T(8,128)(2,1)S(1)}, f32[8,128]{1,0:T(8,128)S(1)}) custom-call(bf16[128,256]{1,0:T(8,128)(2,1)S(1)} %get-tuple-element.35.own_ref, f32[8,128]{1,0:T(8,128)S(1)} %broadcast_in_dim.105.term_ref), custom_call_target="tpu_custom_call" | custom-call | bytes 327680 | tf_op jit(solution)/shard_map/mp_gather_sum/pallas_call | solution.py:340
  122.1 3.4 %convolution_convert_fusion.3.part_ref = bf16[128,1024]{1,0:T(8,128)(2,1)S(1)} fusion(bf16[1024,1024]{1,0:T(8,128)(2,1)S(1)} %copy-done, bf16[1024,1024]{1,0:T(8,128)(2,1)} %param.11, f32[128,1024]{1,0:T(8,128)} %copy-done.8, bf16[128,1024]{1,0:T(8,128)(2,1)S(1)} %get-tuple-element.12, f32[128]{0:T(128)S(1)} %bitcast_multiply_fusion.5, ...), kind=kOutput, calls=%fused_computation.11 | convolution fusion | flops 539099136 | bytes 5506048 | tf_op jit(solution)/shard_map/dot_general | solution.py:426
  125.5 7.4 %mp_scatter.4 = f32[128,256]{1,0:T(8,128)S(1)} custom-call(bf16[128,1024]{1,0:T(8,128)(2,1)S(1)} %convolution_convert_fusion.3.part_ref), custom_call_target="tpu_custom_call" | custom-call | flops 131072 | bytes 524288 | tf_op jit(solution)/shard_map/mp_scatter/pallas_call | solution.py:310
  133.2 1.6 add_convert_fusion.1
  134.8 20.5 %all-to-all-done = bf16[128,16,256]{2,1,0:T(8,128)(2,1)} async-done(((bf16[128,16,256]{2,1,0:T(8,128)(2,1)}), bf16[128,16,256]{2,1,0:T(8,128)(2,1)}, u32[]{:S(2)}, u32[]{:S(2)}) %all-to-all-start) | async-done | bytes 1048608 | tf_op jit(solution)/shard_map/all_to_all | solution.py:513
  155.3 2.1 %multiply_reduce_fusion.1 = (f32[128]{0:T(128)S(1)}, bf16[128,256]{1,0:T(8,128)(2,1)S(1)}, f32[128,256]{1,0:T(8,128)S(1)}) fusion(f32[128,256]{1,0:T(8,128)S(1)} %get-tuple-element.29, f32[128]{0:T(128)S(1)} %copy-done.14, bf16[2048,256]{1,0:T(8,128)(2,1)} %bitcast.12, s32[2048]{0:T(1024)S(1)} %eq.63, f32[128,256]{1,0:T(8,128)S(1)} %copy-done.6, ...), kind=kOutput, calls=%fused_computation.62 | convolution fusion | flops 134676352 | bytes 1517056 | tf_op jit(solution)/shard_map/dot_general | solution.py:524
  157.4 8.4 %mp_gather_sum.3 = (bf16[128,1024]{1,0:T(8,128)(2,1)S(1)}, f32[8,128]{1,0:T(8,128)S(1)}) custom-call(bf16[128,256]{1,0:T(8,128)(2,1)S(1)} %get-tuple-element.33.own_ref, f32[8,128]{1,0:T(8,128)S(1)} %broadcast_in_dim.106.term_ref), custom_call_target="tpu_custom_call" | custom-call | bytes 327680 | tf_op jit(solution)/shard_map/mp_gather_sum/pallas_call | solution.py:340
  165.8 3.2 %convolution_convert_fusion.2.part_ref = bf16[128,1024]{1,0:T(8,128)(2,1)S(1)} fusion(bf16[1024,1024]{1,0:T(8,128)(2,1)S(1)} %copy-done, bf16[1024,1024]{1,0:T(8,128)(2,1)} %param.11, f32[128,1024]{1,0:T(8,128)} %copy-done.7, bf16[128,1024]{1,0:T(8,128)(2,1)S(1)} %get-tuple-element.16, f32[128]{0:T(128)S(1)} %bitcast_multiply_fusion.2, ...), kind=kOutput, calls=%fused_computation.10 | convolution fusion | flops 539099136 | bytes 5506048 | tf_op jit(solution)/shard_map/dot_general | solution.py:426
  169.1 7.3 %mp_scatter.5 = f32[128,256]{1,0:T(8,128)S(1)} custom-call(bf16[128,1024]{1,0:T(8,128)(2,1)S(1)} %convolution_convert_fusion.2.part_ref), custom_call_target="tpu_custom_call" | custom-call | flops 131072 | bytes 524288 | tf_op jit(solution)/shard_map/mp_scatter/pallas_call | solution.py:310
  176.4 0.7 add_convert_fusion
  (63 shorter events, 3.4 us)
Async XLA Ops:
  0.6 1.6 copy-start
  2.2 2.3 %copy-start.3 = (bf16[1024,1024]{1,0:T(8,128)(2,1)S(1)}, bf16[1024,1024]{1,0:T(8,128)(2,1)}, u32[]{:S(2)}) copy-start(bf16[1024,1024]{1,0:T(8,128)(2,1)} %param.11) | copy-start | bytes 6291460
  3.8 0.8 copy-start.7
  4.6 10.0 %copy-start.12 = (s32[1,128,16]{1,2,0:T(8,128)S(1)}, s32[1,128,16]{1,2,0:T(8,128)}, u32[]{:S(2)}) copy-start(s32[1,128,16]{1,2,0:T(8,128)} %param.14) | copy-start | bytes 24580
  4.6 10.2 %copy-start.10 = (bf16[128,1024]{1,0:T(8,128)(2,1)S(1)}, bf16[128,1024]{1,0:T(8,128)(2,1)}, u32[]{:S(2)}) copy-start(bf16[128,1024]{1,0:T(8,128)(2,1)} %param.8) | copy-start | bytes 786436
  14.6 2.6 %copy-start.9 = (bf16[128,256]{1,0:T(8,128)(2,1)}, bf16[128,256]{1,0:T(8,128)(2,1)S(1)}, u32[]{:S(2)}) copy-start(bf16[128,256]{1,0:T(8,128)(2,1)S(1)} %convert_element_type.125) | copy-start | bytes 196612
  14.8 1.8 %copy-start.4 = (bf16[1024,1024]{1,0:T(8,128)(2,1)S(1)}, bf16[1024,1024]{1,0:T(8,128)(2,1)}, u32[]{:S(2)}) copy-start(bf16[1024,1024]{1,0:T(8,128)(2,1)} %param.11) | copy-start | bytes 6291460
  15.3 0.8 copy-start.8
  55.7 17.5 %copy-start.11 = (s32[128,8]{0,1:T(8,128)S(1)}, s32[128,8]{0,1:T(8,128)}, u32[]{:S(2)}) copy-start(s32[128,8]{0,1:T(8,128)} %param.12) | copy-start | bytes 12292
  72.7 39.8 %copy-start.5 = (f32[128,256]{1,0:T(8,128)}, f32[128,256]{1,0:T(8,128)S(1)}, u32[]{:S(2)}) copy-start(f32[128,256]{1,0:T(8,128)S(1)} %get-tuple-element.27) | copy-start | bytes 393220
  72.8 11.2 %copy-start.16 = (s32[128,8]{0,1:T(8,128)S(1)}, s32[128,8]{0,1:T(8,128)}, u32[]{:S(2)}) copy-start(s32[128,8]{0,1:T(8,128)} %param.13) | copy-start | bytes 12292
  89.3 66.1 %all-to-all-start = ((bf16[128,16,256]{2,1,0:T(8,128)(2,1)}), bf16[128,16,256]{2,1,0:T(8,128)(2,1)}, u32[]{:S(2)}, u32[]{:S(2)}) async-start(bf16[128,16,256]{2,1,0:T(8,128)(2,1)} %bitcast.70), calls=%async_computation | async-start | bytes 2097152 | tf_op jit(solution)/shard_map/all_to_all | solution.py:513
  111.9 2.6 %copy-start.1 = (bf16[256,1024]{1,0:T(8,128)(2,1)}, bf16[256,1024]{1,0:T(8,128)(2,1)S(1)}, u32[]{:S(2)}) copy-start(bf16[256,1024]{1,0:T(8,128)(2,1)S(1)} %mp_gather.1) | copy-start | bytes 1572868
  122.1 10.9 %copy-start.13 = (s32[1,128,16]{1,2,0:T(8,128)S(1)}, s32[1,128,16]{1,2,0:T(8,128)}, u32[]{:S(2)}) copy-start(s32[1,128,16]{1,2,0:T(8,128)} %param.14) | copy-start | bytes 24580
  122.1 11.1 %copy-start.6 = (f32[128,256]{1,0:T(8,128)S(1)}, f32[128,256]{1,0:T(8,128)}, u32[]{:S(2)}) copy-start(f32[128,256]{1,0:T(8,128)} %copy-done.5) | copy-start | bytes 393220
  122.1 33.2 %copy-start.14 = (f32[128]{0:T(128)S(1)}, f32[128]{0:T(128)}, u32[]{:S(2)}) copy-start(f32[128]{0:T(128)} %get-tuple-element.36) | copy-start | bytes 1540
  122.1 33.2 %copy-start.17 = (f32[128]{0:T(128)S(1)}, f32[128]{0:T(128)}, u32[]{:S(2)}) copy-start(f32[128]{0:T(128)} %get-tuple-element.22) | copy-start | bytes 1540
  125.5 40.3 %copy-start.2 = (bf16[256,1024]{1,0:T(8,128)(2,1)S(1)}, bf16[256,1024]{1,0:T(8,128)(2,1)}, u32[]{:S(2)}) copy-start(bf16[256,1024]{1,0:T(8,128)(2,1)} %copy-done.1) | copy-start | bytes 1572868
  133.0 32.8 %copy-start.15 = (f32[128]{0:T(128)S(1)}, f32[128]{0:T(128)}, u32[]{:S(2)}) copy-start(f32[128]{0:T(128)} %get-tuple-element.36) | copy-start | bytes 1540

commit v7 on v5

--- a/solution.py
+++ b/solution.py
@@ -407,7 +407,7 @@
         axis=0,
     )
     pre_query, part_query = encode_part(query_states, w_in, w_out)
-    column, sum_query = column_gather(block, part_query, plane, 9, 7)
+    column, sum_query = column_gather(block, part_query, plane, 3, 7)
     out_query = own_columns(query_states).astype(jnp.float32) + sum_query
     start = (lax.axis_index("dp") // plane) * plane * capacity
     served_here = lax.dynamic_slice(

time: 178 us -> 176 us (0.989)
  transfers between devices with their start and end apart: 1 -> 1, of which waited for: 1 -> 1; matrix products, arithmetic and copies ran while one was open for 5% -> 5% of each run, Pallas kernels for 14% -> 15%
where the time goes in v7:
time: 176 us; the launch traced here: 175 us
  Pallas kernels  109 us (62%)
  waiting for transfers between devices  19.5 us (11%)
  matrix products  15.4 us (9%)
  other arithmetic  13.2 us (8%)
  starting transfers between devices  11.1 us (6%)
  local copies, waits for them, and re-layouts  5.03 us (3%)
  between operations  1.82 us (1%)
    pallas_call x1, Pallas kernels, column_gather(): pl.pallas_call(functools.partial(column_kernel, ways, plane, parts), out_...  37.6 us
    pallas_call x3, Pallas kernels, mp_scatter(): pl.pallas_call(functools.partial(scatter_kernel, ways), out_shape=jax.Sha...  23.2 us
    all_to_all x1, waiting for transfers between devices, shards(): lax.all_to_all(outgoing_grad.reshape(owners, capacity, column_width), 'dp...  19.5 us
    pallas_call x2, Pallas kernels, mp_gather_sum(): pl.pallas_call(functools.partial(gather_sum_kernel, ways), out_shape=(jax...  15.8 us
    pallas_call x1, Pallas kernels, plane_exchange(): pl.pallas_call(functools.partial(plane_kernel, plane, capacity), out_shap...  15.8 us
    all_to_all x1, starting transfers between devices, shards(): lax.all_to_all(outgoing_grad.reshape(owners, capacity, column_width), 'dp...  11.1 us
    pallas_call x1, Pallas kernels, mp_gather(): pl.pallas_call(functools.partial(gather_kernel, ways), out_shape=jax.Shap...  10.6 us
    dot_general x2, matrix products, decode(): lax.dot_general(grad_pre, w_in, contract, preferred_element_type=jnp.floa...  6.63 us
  transfers between devices with their start and end apart: 1, of which 1 were waited for; matrix products, arithmetic and copies ran while one was open for 5% of the time, Pallas kernels for 15%

profile of v7, /device:TPU:32, one launch (start us, length us, event | category | flops | bytes accessed | tf_op | source)
XLA Modules:
  0.0 175.1 jit_solution(7269557841599011696)
XLA Ops:
  0.7 1.5 copy-done
  2.2 1.5 fusion.56
  3.8 0.8 copy-done.7
  5.1 8.5 %mp_scatter.3 = f32[128,256]{1,0:T(8,128)S(1)} custom-call(bf16[128,1024]{1,0:T(8,128)(2,1)S(1)} %convolution_convert_fusion.5.part_ref), custom_call_target="tpu_custom_call" | custom-call | flops 131072 | bytes 524288 | tf_op jit(solution)/shard_map/mp_scatter/pallas_call | solution.py:262
  13.6 1.0 multiply_reduce_fusion.4
  15.3 0.8 copy-done.8
  17.3 37.6 %column_gather.1 = (bf16[16,144,256]{2,1,0:T(8,128)(2,1)S(1)}, f32[128,256]{1,0:T(8,128)S(1)}) custom-call(bf16[144,256]{1,0:T(8,128)(2,1)S(1)} %maximum_maximum_fusion.block_ref, bf16[128,1024]{1,0:T(8,128)(2,1)S(1)} %convolution_convert_fusion.4.part_ref), custom_call_target="tpu_custom_call" | custom-call | tf_op jit(solution)/shard_map/column_gather/pallas_call | solution.py:327
  54.9 0.7 convolution_convert_fusion.1.rows_ref
  55.7 15.8 %plane_exchange.1 = bf16[16,128,256]{2,1,0:T(8,128)(2,1)S(1)} custom-call(bf16[16,128,256]{2,1,0:T(8,128)(2,1)S(1)} %convolution_convert_fusion.1.rows_ref), custom_call_target="tpu_custom_call" | custom-call | tf_op jit(solution)/shard_map/plane_exchange/pallas_call | solution.py:345
  71.5 1.0 multiply_reduce_fusion.3
  74.2 2.8 %select_reduce_fusion.2 = (f32[8,128]{1,0:T(8,128)S(1)}, f32[8,128]{1,0:T(8,128)S(1)}) fusion(f32[2048]{0:T(1024)S(1)} %bitcast.73, s32[8,128]{1,0:T(8,128)S(1)} %convert_add_fusion.2, f32[128,2048]{1,0:T(8,128)S(1)} %fusion.58), kind=kLoop, calls=%fused_computation.2 | loop fusion | flops 10483712 | bytes 1069056 | tf_op jit(solution)/shard_map/reduce_sum | solution.py:442
  77.0 6.1 %mp_sum.1 = f32[24,128]{1,0:T(8,128)S(1)} custom-call(f32[24,128]{1,0:T(8,128)S(1)} %concatenate.10.term_ref), custom_call_target="tpu_custom_call" | custom-call | bytes 61440 | tf_op jit(solution)/shard_map/mp_sum/pallas_call | solution.py:309
  83.9 0.6 fusion.54
  84.4 1.4 select_reduce_fusion.1
  85.8 1.5 convolution_convert_fusion
  87.3 11.1 %all-to-all-start = ((bf16[128,16,256]{2,1,0:T(8,128)(2,1)}), bf16[128,16,256]{2,1,0:T(8,128)(2,1)}, u32[]{:S(2)}, u32[]{:S(2)}) async-start(bf16[128,16,256]{2,1,0:T(8,128)(2,1)} %bitcast.70), calls=%async_computation | async-start | bytes 2097152 | tf_op jit(solution)/shard_map/all_to_all | solution.py:465
  98.4 0.9 pad_maximum_fusion.own_ref
  99.3 10.6 %mp_gather.1 = bf16[256,1024]{1,0:T(8,128)(2,1)S(1)} custom-call(bf16[256,256]{1,0:T(8,128)(2,1)S(1)} %pad_maximum_fusion.own_ref), custom_call_target="tpu_custom_call" | custom-call | bytes 655360 | tf_op jit(solution)/shard_map/mp_gather/pallas_call | solution.py:277
  109.9 0.8 copy-done.1
  110.7 0.5 bitcast_multiply_fusion.4
  111.2 1.4 select_reduce_fusion
  112.7 1.0 multiply_reduce_fusion.2
  113.6 7.5 %mp_gather_sum.2 = (bf16[128,1024]{1,0:T(8,128)(2,1)S(1)}, f32[8,128]{1,0:T(8,128)S(1)}) custom-call(bf16[128,256]{1,0:T(8,128)(2,1)S(1)} %get-tuple-element.37.own_ref, f32[8,128]{1,0:T(8,128)S(1)} %broadcast_in_dim.105.term_ref), custom_call_target="tpu_custom_call" | custom-call | bytes 327680 | tf_op jit(solution)/shard_map/mp_gather_sum/pallas_call | solution.py:292
  121.1 3.4 %convolution_convert_fusion.3.part_ref = bf16[128,1024]{1,0:T(8,128)(2,1)S(1)} fusion(bf16[1024,1024]{1,0:T(8,128)(2,1)S(1)} %copy-done, bf16[1024,1024]{1,0:T(8,128)(2,1)} %param.11, f32[128,1024]{1,0:T(8,128)} %copy-done.8, bf16[128,1024]{1,0:T(8,128)(2,1)S(1)} %get-tuple-element.16, f32[128]{0:T(128)S(1)} %bitcast_multiply_fusion.5, ...), kind=kOutput, calls=%fused_computation.11 | convolution fusion | flops 539099136 | bytes 5506048 | tf_op jit(solution)/shard_map/dot_general | solution.py:377
  124.5 7.4 %mp_scatter.4 = f32[128,256]{1,0:T(8,128)S(1)} custom-call(bf16[128,1024]{1,0:T(8,128)(2,1)S(1)} %convolution_convert_fusion.3.part_ref), custom_call_target="tpu_custom_call" | custom-call | flops 131072 | bytes 524288 | tf_op jit(solution)/shard_map/mp_scatter/pallas_call | solution.py:262
  132.2 1.6 add_convert_fusion.1
  133.8 19.5 %all-to-all-done = bf16[128,16,256]{2,1,0:T(8,128)(2,1)} async-done(((bf16[128,16,256]{2,1,0:T(8,128)(2,1)}), bf16[128,16,256]{2,1,0:T(8,128)(2,1)}, u32[]{:S(2)}, u32[]{:S(2)}) %all-to-all-start) | async-done | bytes 1048608 | tf_op jit(solution)/shard_map/all_to_all | solution.py:465
  153.3 2.1 %multiply_reduce_fusion.1 = (f32[128]{0:T(128)S(1)}, bf16[128,256]{1,0:T(8,128)(2,1)S(1)}, f32[128,256]{1,0:T(8,128)S(1)}) fusion(f32[128,256]{1,0:T(8,128)S(1)} %get-tuple-element.31, f32[128]{0:T(128)S(1)} %copy-done.14, bf16[2048,256]{1,0:T(8,128)(2,1)} %bitcast.12, s32[2048]{0:T(1024)S(1)} %eq.63, f32[128,256]{1,0:T(8,128)S(1)} %copy-done.6, ...), kind=kOutput, calls=%fused_computation.62 | convolution fusion | flops 134676352 | bytes 1517056 | tf_op jit(solution)/shard_map/dot_general | solution.py:476
  155.4 8.4 %mp_gather_sum.3 = (bf16[128,1024]{1,0:T(8,128)(2,1)S(1)}, f32[8,128]{1,0:T(8,128)S(1)}) custom-call(bf16[128,256]{1,0:T(8,128)(2,1)S(1)} %get-tuple-element.35.own_ref, f32[8,128]{1,0:T(8,128)S(1)} %broadcast_in_dim.106.term_ref), custom_call_target="tpu_custom_call" | custom-call | bytes 327680 | tf_op jit(solution)/shard_map/mp_gather_sum/pallas_call | solution.py:292
  163.8 3.2 %convolution_convert_fusion.2.part_ref = bf16[128,1024]{1,0:T(8,128)(2,1)S(1)} fusion(bf16[1024,1024]{1,0:T(8,128)(2,1)S(1)} %copy-done, bf16[1024,1024]{1,0:T(8,128)(2,1)} %param.11, f32[128,1024]{1,0:T(8,128)} %copy-done.7, bf16[128,1024]{1,0:T(8,128)(2,1)S(1)} %get-tuple-element.20, f32[128]{0:T(128)S(1)} %bitcast_multiply_fusion.2, ...), kind=kOutput, calls=%fused_computation.10 | convolution fusion | flops 539099136 | bytes 5506048 | tf_op jit(solution)/shard_map/dot_general | solution.py:377
  167.0 7.3 %mp_scatter.5 = f32[128,256]{1,0:T(8,128)S(1)} custom-call(bf16[128,1024]{1,0:T(8,128)(2,1)S(1)} %convolution_convert_fusion.2.part_ref), custom_call_target="tpu_custom_call" | custom-call | flops 131072 | bytes 524288 | tf_op jit(solution)/shard_map/mp_scatter/pallas_call | solution.py:262
  174.3 0.7 add_convert_fusion
  (64 shorter events, 4.4 us)
Async XLA Ops:
  0.6 1.6 copy-start
  2.2 2.3 %copy-start.3 = (bf16[1024,1024]{1,0:T(8,128)(2,1)S(1)}, bf16[1024,1024]{1,0:T(8,128)(2,1)}, u32[]{:S(2)}) copy-start(bf16[1024,1024]{1,0:T(8,128)(2,1)} %param.11) | copy-start | bytes 6291460
  3.8 0.8 copy-start.7
  4.6 10.0 %copy-start.12 = (s32[1,128,16]{1,2,0:T(8,128)S(1)}, s32[1,128,16]{1,2,0:T(8,128)}, u32[]{:S(2)}) copy-start(s32[1,128,16]{1,2,0:T(8,128)} %param.14) | copy-start | bytes 24580
  4.6 10.2 %copy-start.10 = (bf16[128,1024]{1,0:T(8,128)(2,1)S(1)}, bf16[128,1024]{1,0:T(8,128)(2,1)}, u32[]{:S(2)}) copy-start(bf16[128,1024]{1,0:T(8,128)(2,1)} %param.8) | copy-start | bytes 786436
  14.6 2.6 %copy-start.9 = (bf16[128,256]{1,0:T(8,128)(2,1)}, bf16[128,256]{1,0:T(8,128)(2,1)S(1)}, u32[]{:S(2)}) copy-start(bf16[128,256]{1,0:T(8,128)(2,1)S(1)} %convert_element_type.125) | copy-start | bytes 196612
  14.8 1.8 %copy-start.4 = (bf16[1024,1024]{1,0:T(8,128)(2,1)S(1)}, bf16[1024,1024]{1,0:T(8,128)(2,1)}, u32[]{:S(2)}) copy-start(bf16[1024,1024]{1,0:T(8,128)(2,1)} %param.11) | copy-start | bytes 6291460
  15.3 0.8 copy-start.8
  55.7 17.3 %copy-start.11 = (s32[128,8]{0,1:T(8,128)S(1)}, s32[128,8]{0,1:T(8,128)}, u32[]{:S(2)}) copy-start(s32[128,8]{0,1:T(8,128)} %param.12) | copy-start | bytes 12292
  72.4 40.2 %copy-start.5 = (f32[128,256]{1,0:T(8,128)}, f32[128,256]{1,0:T(8,128)S(1)}, u32[]{:S(2)}) copy-start(f32[128,256]{1,0:T(8,128)S(1)} %get-tuple-element.29) | copy-start | bytes 393220
  72.6 11.3 %copy-start.16 = (s32[128,8]{0,1:T(8,128)S(1)}, s32[128,8]{0,1:T(8,128)}, u32[]{:S(2)}) copy-start(s32[128,8]{0,1:T(8,128)} %param.13) | copy-start | bytes 12292
  87.3 66.0 %all-to-all-start = ((bf16[128,16,256]{2,1,0:T(8,128)(2,1)}), bf16[128,16,256]{2,1,0:T(8,128)(2,1)}, u32[]{:S(2)}, u32[]{:S(2)}) async-start(bf16[128,16,256]{2,1,0:T(8,128)(2,1)} %bitcast.70), calls=%async_computation | async-start | bytes 2097152 | tf_op jit(solution)/shard_map/all_to_all | solution.py:465
  109.9 0.8 copy-start.1
  121.1 10.9 %copy-start.13 = (s32[1,128,16]{1,2,0:T(8,128)S(1)}, s32[1,128,16]{1,2,0:T(8,128)}, u32[]{:S(2)}) copy-start(s32[1,128,16]{1,2,0:T(8,128)} %param.14) | copy-start | bytes 24580
  121.1 11.1 %copy-start.6 = (f32[128,256]{1,0:T(8,128)S(1)}, f32[128,256]{1,0:T(8,128)}, u32[]{:S(2)}) copy-start(f32[128,256]{1,0:T(8,128)} %copy-done.5) | copy-start | bytes 393220
  121.1 32.2 %copy-start.14 = (f32[128]{0:T(128)S(1)}, f32[128]{0:T(128)}, u32[]{:S(2)}) copy-start(f32[128]{0:T(128)} %get-tuple-element.38) | copy-start | bytes 1540
  121.1 32.2 %copy-start.17 = (f32[128]{0:T(128)S(1)}, f32[128]{0:T(128)}, u32[]{:S(2)}) copy-start(f32[128]{0:T(128)} %get-tuple-element.24) | copy-start | bytes 1540
  124.5 39.2 %copy-start.2 = (bf16[256,1024]{1,0:T(8,128)(2,1)S(1)}, bf16[256,1024]{1,0:T(8,128)(2,1)}, u32[]{:S(2)}) copy-start(bf16[256,1024]{1,0:T(8,128)(2,1)} %copy-done.1) | copy-start | bytes 1572868
  132.0 31.8 %copy-start.15 = (f32[128]{0:T(128)S(1)}, f32[128]{0:T(128)}, u32[]{:S(2)}) copy-start(f32[128]{0:T(128)} %get-tuple-element.38) | copy-start | bytes 1540
